TPU v7x, 128 devices: a whole 4x4x4 slice. The times are simulated.
128 devices in a mesh: brick: 8 (over z, core), view: 16 (over y, x).
Axes of the slice: x: 4, y: 4, z: 4, core: 2. Of those that a mesh axis runs over, the one named last changes fastest.
Arguments:
- latent_grid: bfloat16 [8, 16, 32768], P('brick'), may hold values from -6 to 6
- layer_one: bfloat16 [64, 16], replicated, may hold values from -1.5 to 1.5
- layer_two: bfloat16 [64, 64], replicated, may hold values from -0.75 to 0.75
- layer_three: bfloat16 [64, 64], replicated, may hold values from -0.75 to 0.75
- layer_four: bfloat16 [33, 64], replicated, may hold values from -0.75 to 0.75
- view_order: int32 [16], P('view'), may hold values from 0 to 7
- samples: int32 [16, 8, 8, 4096], P('view', 'brick'), may hold values from 0 to 32767, as said below
- pixel_grad: float32 [16, 32, 4096], P('view', None, 'brick'), may hold values from -24 to 24
Outputs:
- composite: float32 [16, 32, 4096], P('view', None, 'brick')
- latent_grad: float32 [8, 16, 32768], P('brick')
- layer_one_grad: float32 [64, 16], replicated
- layer_two_grad: float32 [64, 64], replicated
- layer_three_grad: float32 [64, 64], replicated
- layer_four_grad: float32 [33, 64], replicated
Inputs may be any that keep to these rules, and one draw needn't show every extreme that they name: The depth rank of brick b in view v is b xor view_order[v]. `samples`: sample step s of pixel p reads a voxel from s * 4096 + (p // 512) * 512 to that plus 512 - 1.
All inputs are finite; a program needn't handle non-finite values.
Results may differ from a plain program's by a relative error of at most 0.015.
Values sent between devices are 32-bit elements; how exact they have to be, the bound alone decides.
No kernel may reach another device: no remote copies, remote signals or barrier semaphores. Data moves between devices by JAX's collectives and lax.ppermute only.
A program may use at most 128 MiB of HBM per device.

v0:
```python
import functools

import jax
import jax.numpy as jnp
from jax import lax
from jax.experimental import pallas as pl
from jax.experimental.pallas import tpu as pltpu
from jax.sharding import PartitionSpec as P


F32 = jnp.float32
BF16 = jnp.bfloat16
NT = (((1,), (1,)), ((), ()))
STEPS = 8
TILE = 512
LANES = 128
PARTS = TILE // LANES
OUT_ROWS = 40


def mm(a, b):
    return jnp.dot(a, b, preferred_element_type=F32)


def mm_nt(a, b):
    return lax.dot_general(a, b, NT, preferred_element_type=F32)


def place_to_tile(place, brick):
    return jnp.bitwise_xor(jnp.bitwise_xor(place, jnp.right_shift(place, 2) * 2), brick)


def one_hot(local):
    low = jnp.bitwise_and(local, LANES - 1)
    rows = lax.broadcasted_iota(jnp.int32, (LANES, local.shape[1]), 0)
    return jnp.where(rows == low, 1.0, 0.0).astype(BF16)


def row_of(array, step):
    return array[step : step + 1, :]


def colour_at(colour_ref, step):
    return colour_ref[0, :, step * TILE : (step + 1) * TILE].astype(F32)


def forward_kernel(
    first, brick_ref, grid_ref, samples_ref, one_ref, two_ref, three_ref, four_ref,
    partial_ref, trans_ref, hidden_ref, feature_ref, colour_ref, ray_ref, last_ref,
):
    tile = place_to_tile(pl.program_id(0) + first, brick_ref[0])
    spacing = 2.0 / (STEPS * 8)
    channels = grid_ref.shape[0]
    row = pl.program_id(0)
    for step in range(STEPS):
        span = pl.ds(step * TILE, TILE)
        local = jnp.bitwise_and(samples_ref[step : step + 1, :], TILE - 1)
        base = step * (grid_ref.shape[1] // STEPS) + tile * TILE
        pieces = [
            grid_ref[:, pl.ds(pl.multiple_of(base + k * LANES, LANES), LANES)]
            for k in range(PARTS)
        ]
        wide = mm(jnp.concatenate(pieces, axis=0), one_hot(local))
        high = jnp.broadcast_to(jnp.right_shift(local, 7), (channels, TILE))
        picked = wide[:channels]
        for k in range(1, PARTS):
            picked = jnp.where(high == k, wide[k * channels : (k + 1) * channels], picked)
        feature_ref[0, :, span] = picked.astype(BF16)
    for layer, weight_ref in enumerate((one_ref, two_ref, three_ref)):
        for step in range(STEPS):
            span = pl.ds(step * TILE, TILE)
            value = feature_ref[0, :, span] if layer == 0 else hidden_ref[0, layer - 1, :, span]
            half = mm(weight_ref[...], value)
            gate = 1.0 + jnp.tanh(half)
            hidden = half * gate
            hidden = hidden.astype(BF16)
            gate = gate.astype(BF16)
            hidden_ref[0, layer, :, span] = hidden
            hidden_ref[0, 3 + layer, :, span] = gate + hidden * (2.0 - gate)
    for step in range(STEPS):
        span = pl.ds(step * TILE, TILE)
        output = mm(four_ref[...], hidden_ref[0, 2, :, span])
        colour_ref[0, :, span] = (0.5 + 0.5 * jnp.tanh(output[:32])).astype(BF16)
        last_ref[step : step + 1, :] = output[32:33]
    half = last_ref[...]
    raw = half + half
    depth = (jnp.maximum(raw, 0.0) + jnp.log1p(jnp.exp(-jnp.abs(raw)))) * spacing
    running = [row_of(depth, 0)]
    for step in range(1, STEPS):
        running.append(running[-1] + row_of(depth, step))
    earlier = jnp.concatenate([jnp.zeros_like(running[0])] + running[:-1], axis=0)
    running = jnp.concatenate(running, axis=0)
    through = jnp.exp(-running)
    small = depth * (1.0 - depth * (0.5 - depth * (1.0 / 6.0 - depth * (1.0 / 24.0))))
    absorbed = jnp.where(depth < 0.02, small, 1.0 - jnp.exp(-depth))
    factor = jnp.exp(-earlier) * absorbed
    ray_ref[0, 0] = factor
    ray_ref[0, 1] = through
    ray_ref[0, 2] = spacing * (0.5 + 0.5 * jnp.tanh(half))
    image = row_of(factor, 0) * colour_at(colour_ref, 0)
    for step in range(1, STEPS):
        image = image + row_of(factor, step) * colour_at(colour_ref, step)
    partial_ref[0] = image
    trans_ref[pl.ds(row, 1), :] = through[STEPS - 1 : STEPS, :]


def backward_kernel(
    first, brick_ref, samples_ref, given_ref, weight_ref, behind_ref, hidden_ref, feature_ref,
    colour_ref, ray_ref, one_t_ref, two_t_ref, three_t_ref, four_t_ref, before_ref,
    grid_ref, packed_ref, cot_ref, out_ref, feature_cot_ref,
):
    place = pl.program_id(0) + first
    channels = feature_ref.shape[1]

    @pl.when(pl.program_id(0) == 0)
    def _():
        if first == 0:
            packed_ref[...] = jnp.zeros_like(packed_ref)
        else:
            packed_ref[...] = before_ref[...]

    weight = weight_ref[pl.ds(place, 1), :]
    trans_grad = weight * behind_ref[pl.ds(place, 1), :]
    factor = ray_ref[0, 0]
    through = ray_ref[0, 1]
    scaled = weight * given_ref[0]
    dots = jnp.concatenate(
        [
            jnp.sum(scaled * colour_at(colour_ref, step), axis=0, keepdims=True)
            for step in range(STEPS)
        ],
        axis=0,
    )
    taken = factor * dots
    later = [row_of(through, STEPS - 1) * trans_grad]
    for step in range(STEPS - 1, 0, -1):
        later.append(later[-1] + row_of(taken, step))
    depth_grad = through * dots - jnp.concatenate(later[::-1], axis=0)
    last = depth_grad * ray_ref[0, 2]
    first_row = lax.broadcasted_iota(jnp.int32, (OUT_ROWS - 32, TILE), 0) == 0
    for step in range(STEPS):
        span = pl.ds(step * TILE, TILE)
        colour = colour_at(colour_ref, step)
        out_ref[:, span] = jnp.concatenate(
            [
                (colour - colour * colour) * (row_of(factor, step) * scaled),
                jnp.where(first_row, row_of(last, step), 0.0),
            ],
            axis=0,
        ).astype(BF16)
    sums = [0.0] * 4
    for layer in (2, 1, 0):
        for step in range(STEPS):
            span = pl.ds(step * TILE, TILE)
            weight_t = (two_t_ref, three_t_ref, four_t_ref)[layer][...]
            cot = out_ref[:, span] if layer == 2 else cot_ref[layer + 1, :, span]
            cot_ref[layer, :, span] = (
                mm(weight_t, cot).astype(BF16) * hidden_ref[0, 3 + layer, :, span]
            )
            if step % 2 == 1:
                pair = pl.ds((step - 1) * TILE, 2 * TILE)
                cot = out_ref[:, pair] if layer == 2 else cot_ref[layer + 1, :, pair]
                sums[layer + 1] += mm_nt(cot, hidden_ref[0, layer, :, pair])
    for step in range(STEPS):
        span = pl.ds(step * TILE, TILE)
        feature_cot_ref[:, span] = mm(one_t_ref[...], cot_ref[0, :, span]).astype(BF16)
        if step % 2 == 1:
            pair = pl.ds((step - 1) * TILE, 2 * TILE)
            sums[0] += mm_nt(feature_ref[0, :, pair], cot_ref[0, :, pair])
    for step in range(STEPS):
        feature_cot = feature_cot_ref[:, pl.ds(step * TILE, TILE)].astype(F32)
        local = jnp.bitwise_and(samples_ref[step : step + 1, :], TILE - 1)
        high = jnp.broadcast_to(jnp.right_shift(local, 7), (channels, TILE))
        spread = jnp.concatenate(
            [jnp.where(high == k, feature_cot, 0.0) for k in range(PARTS)], axis=0
        ).astype(BF16)
        half = jnp.bitwise_xor(step // 4, brick_ref[6 + first // 2])
        grid_ref[0, half * 4 + step % 4] = mm_nt(spread, one_hot(local))

    for half in range(2):
        rows = slice(32 * half, 32 * half + 32)
        packed_ref[0, :, 128 * half : 128 * half + 64] += 0.5 * sums[1][rows]
        packed_ref[0, :, 128 * half + 64 : 128 * half + 128] += 0.5 * sums[2][rows]
    packed_ref[0, :, 256:320] += sums[3][0:32]
    packed_ref[0, 0:8, 384:448] += sums[3][32:40]
    packed_ref[0, 0:16, 320:384] += 0.5 * sums[0]


def prepare_kernel(
    grid_in_ref, samples_in_ref, one_t_in_ref, two_in_ref, three_in_ref, four_in_ref,
    grid_ref, samples_ref, one_ref, two_ref, three_ref, four_ref,
    one_t_ref, two_t_ref, three_t_ref, four_t_ref,
):
    grid_ref[...] = grid_in_ref[...]
    samples_ref[...] = samples_in_ref[...]
    one_t = one_t_in_ref[...].astype(F32) * 0.5
    one_ref[...] = one_t.T.astype(BF16)
    one_t_ref[...] = one_t.astype(BF16)
    for in_ref, plain_ref, turned_ref in (
        (two_in_ref, two_ref, two_t_ref),
        (three_in_ref, three_ref, three_t_ref),
    ):
        layer = in_ref[...].astype(F32) * 0.5
        plain_ref[...] = layer.astype(BF16)
        turned_ref[...] = layer.T.astype(BF16)
    four = four_in_ref[...].astype(F32)
    four = jnp.concatenate([four, jnp.zeros((OUT_ROWS - four.shape[0], 64), F32)], axis=0)
    four_ref[...] = (four * 0.5).astype(BF16)
    four_t_ref[...] = four.T.astype(BF16)


def flip_rows(array, flip):
    if flip == 4:
        return pltpu.roll(array, 4, 0)
    rows = lax.broadcasted_iota(jnp.int32, array.shape, 0)
    upper = jnp.bitwise_and(rows, flip) == 0
    return jnp.where(upper, pltpu.roll(array, 8 - flip, 0), pltpu.roll(array, flip, 0))


def dots_kernel(near_ref, far_ref, part_near_ref, part_far_ref, trans_near_ref, trans_far_ref, out_ref):
    out_ref[0, 0:4, :] = trans_near_ref[...]
    out_ref[0, 4:8, :] = trans_far_ref[...]
    for half, (given_ref, part_ref) in enumerate(
        ((near_ref, part_near_ref), (far_ref, part_far_ref))
    ):
        for p in range(4):
            row = 4 * half + p
            out_ref[1, row : row + 1, :] = jnp.sum(
                given_ref[p] * part_ref[p], axis=0, keepdims=True
            )


def merge_kernel(level, flip, info_ref, own_ref, got_ref, *refs):
    total, dots = own_ref[0], own_ref[1]
    got_total = flip_rows(got_ref[0], flip)
    got_dots = flip_rows(got_ref[1], flip)
    bit = jnp.bitwise_and(jnp.right_shift(info_ref[1], level), 1)
    first = jnp.full(total.shape, bit, jnp.int32) == 0
    if level == 0:
        front, after, behind = jnp.ones_like(total), jnp.ones_like(total), jnp.zeros_like(total)
    else:
        state_ref, *refs = refs
        front, after, behind = state_ref[0], state_ref[1], state_ref[2]
    behind = jnp.where(first, behind + after * got_dots, behind)
    front = jnp.where(first, front, front * got_total)
    if level < 2:
        out_ref, next_ref = refs
        next_ref[0] = front
        next_ref[1] = jnp.where(first, after * got_total, after)
        next_ref[2] = behind
        out_ref[0] = total * got_total
        out_ref[1] = jnp.where(first, dots + total * got_dots, got_dots + got_total * dots)
    else:
        part_near_ref, part_far_ref, front_ref, behind_ref, image_near_ref, image_far_ref = refs
        front_ref[...] = front
        behind_ref[...] = behind
        for p in range(4):
            image_near_ref[p] = front[p : p + 1] * part_near_ref[p]
            image_far_ref[p] = front[p + 4 : p + 5] * part_far_ref[p]


def finish_kernel(info_ref, *refs):
    sources, (packed_in_ref, grid_ref, one_t_ref, two_ref, three_ref, four_ref) = refs[:12], refs[12:]
    channels = grid_ref.shape[1]
    slab = grid_ref.shape[2] // STEPS

    rows = 4 * PARTS * channels
    for colour in range(4):
        bit = info_ref[2 + colour]
        for part in range(4):
            source = sources[3 * colour + min(part, 2)]
            skip = rows if part == 3 else 0
            tile = place_to_tile(2 * colour + jnp.bitwise_xor(bit, part // 2), info_ref[0])
            half = jnp.bitwise_xor(info_ref[6 + colour], part % 2)
            for step in range(4):
                for k in range(PARTS):
                    base = (half * 4 + step) * slab + tile * TILE + k * LANES
                    row = skip + (step * PARTS + k) * channels
                    grid_ref[0, :, pl.ds(pl.multiple_of(base, LANES), LANES)] = source[
                        row : row + channels, :
                    ]
    packed_in_ref = packed_in_ref[...] + sources[11][2 * rows :, :]
    one_t_ref[...] = packed_in_ref[64:80, 64:128]
    two_ref[...] = packed_in_ref[0:64, 0:64]
    three_ref[...] = packed_in_ref[0:64, 64:128]
    four_ref[...] = packed_in_ref[64:97, 0:64]


VMEM = pl.BlockSpec(memory_space=pltpu.VMEM)
SMEM = pl.BlockSpec(memory_space=pltpu.SMEM)
SMALL = pltpu.CompilerParams(vmem_limit_bytes=4 * 2**20)


def run_prepare(grid, samples, one_t, two, three, four):
    channels = one_t.shape[0]
    shapes = [(64, channels), (64, 64), (64, 64), (OUT_ROWS, 64)]
    shapes += [shape[::-1] for shape in shapes]
    return pl.pallas_call(
        prepare_kernel,
        out_shape=[
            jax.ShapeDtypeStruct(grid.shape, grid.dtype),
            jax.ShapeDtypeStruct(samples.shape, samples.dtype),
            *[jax.ShapeDtypeStruct(shape, BF16) for shape in shapes],
        ],
        in_specs=[VMEM] * 6,
        out_specs=[VMEM] * 10,
        compiler_params=SMALL,
        name="prepare",
    )(grid, samples, one_t, two, three, four)


def run_dots(*arrays):
    return pl.pallas_call(
        dots_kernel,
        out_shape=jax.ShapeDtypeStruct((2, 8, TILE), F32),
        in_specs=[VMEM] * 6,
        out_specs=VMEM,
        compiler_params=SMALL,
        name="dots",
    )(*arrays)


def run_merge(level, flip, info, own, got, *more):
    shapes = {
        False: [(2, 8, TILE), (3, 8, TILE)],
        True: [(8, TILE), (8, TILE), (4, 32, TILE), (4, 32, TILE)],
    }[level == 2]
    return pl.pallas_call(
        functools.partial(merge_kernel, level, flip),
        out_shape=[jax.ShapeDtypeStruct(shape, F32) for shape in shapes],
        in_specs=[SMEM] + [VMEM] * (2 + len(more)),
        out_specs=[VMEM] * len(shapes),
        compiler_params=SMALL,
        name="merge",
    )(info, own, got, *more)


def whole(shape):
    return pl.BlockSpec(shape, lambda p, brick: (0,) * len(shape))


def at_place(shape):
    return pl.BlockSpec((1,) + shape, lambda p, brick: (p,) + (0,) * len(shape))


def run_forward(first, brick, grid, samples, one, two, three, four):
    count = 4
    wide = STEPS * TILE
    channels = grid.shape[0]
    shapes = [
        jax.ShapeDtypeStruct((count, 32, TILE), F32),
        jax.ShapeDtypeStruct((count, TILE), F32),
        jax.ShapeDtypeStruct((count, 6, 64, wide), BF16),
        jax.ShapeDtypeStruct((count, channels, wide), BF16),
        jax.ShapeDtypeStruct((count, 32, wide), BF16),
        jax.ShapeDtypeStruct((count, 3, STEPS, TILE), F32),
    ]
    return pl.pallas_call(
        functools.partial(forward_kernel, first),
        out_shape=shapes,
        grid_spec=pltpu.PrefetchScalarGridSpec(
            num_scalar_prefetch=1,
            grid=(count,),
            in_specs=[
                whole(grid.shape),
                pl.BlockSpec(
                    (STEPS, TILE), lambda p, brick: (0, place_to_tile(p + first, brick[0]))
                ),
                whole(one.shape),
                whole(two.shape),
                whole(three.shape),
                whole(four.shape),
            ],
            out_specs=[
                at_place((32, TILE)),
                whole((count, TILE)),
                at_place((6, 64, wide)),
                at_place((channels, wide)),
                at_place((32, wide)),
                at_place((3, STEPS, TILE)),
            ],
            scratch_shapes=[pltpu.VMEM((STEPS, TILE), F32)],
        ),
        cost_estimate=pl.CostEstimate(
            flops=1_000_000_000, bytes_accessed=16_000_000, transcendentals=4_000_000
        ),
        compiler_params=pltpu.CompilerParams(vmem_limit_bytes=14 * 2**20),
        name="forward",
    )(brick, grid, samples, one, two, three, four)


def run_backward(first, brick, samples, given, weight, behind, saved, layers, before):
    count = 2
    skip = first % 4
    wide = STEPS * TILE
    hidden, feature, colour, ray = saved
    channels = feature.shape[1]

    def later(shape):
        return pl.BlockSpec((1,) + shape, lambda p, brick: (p + skip,) + (0,) * len(shape))

    return pl.pallas_call(
        functools.partial(backward_kernel, first),
        out_shape=[
            jax.ShapeDtypeStruct((count, STEPS, PARTS * channels, LANES), F32),
            jax.ShapeDtypeStruct((1, 32, TILE), F32),
        ],
        grid_spec=pltpu.PrefetchScalarGridSpec(
            num_scalar_prefetch=1,
            grid=(count,),
            in_specs=[
                pl.BlockSpec(
                    (STEPS, TILE), lambda p, brick: (0, place_to_tile(p + first, brick[0]))
                ),
                later((32, TILE)),
                whole(weight.shape),
                whole(behind.shape),
                later((6, 64, wide)),
                later((channels, wide)),
                later((32, wide)),
                later((3, STEPS, TILE)),
                *[whole(layer.shape) for layer in layers],
                whole((1, 32, TILE)),
            ],
            out_specs=[
                pl.BlockSpec(
                    (1, STEPS, PARTS * channels, LANES),
                    lambda p, brick: (jnp.bitwise_xor(p, brick[2 + first // 2]), 0, 0, 0),
                ),
                whole((1, 32, TILE)),
            ],
            scratch_shapes=[
                pltpu.VMEM((3, 64, wide), BF16),
                pltpu.VMEM((OUT_ROWS, wide), BF16),
                pltpu.VMEM((channels, wide), BF16),
            ],
        ),
        cost_estimate=pl.CostEstimate(
            flops=1_000_000_000, bytes_accessed=9_000_000, transcendentals=0
        ),
        compiler_params=pltpu.CompilerParams(vmem_limit_bytes=14 * 2**20),
        name="backward",
    )(brick, samples, given, weight, behind, hidden, feature, colour, ray, *layers, before)


def run_finish(info, sources, packed, channels, voxels):
    return pl.pallas_call(
        finish_kernel,
        out_shape=[
            jax.ShapeDtypeStruct((1, channels, voxels), F32),
            jax.ShapeDtypeStruct((channels, 64), F32),
            jax.ShapeDtypeStruct((64, 64), F32),
            jax.ShapeDtypeStruct((64, 64), F32),
            jax.ShapeDtypeStruct((33, 64), F32),
        ],
        in_specs=[SMEM] + [VMEM] * 13,
        out_specs=[VMEM] * 5,
        compiler_params=pltpu.CompilerParams(vmem_limit_bytes=14 * 2**20),
        name="finish",
    )(info, *sources, packed)


def swap_brick(array, flip):
    return lax.ppermute(array, "brick", [(i, i ^ flip) for i in range(8)])


def link_of(colour, turn, odd):
    return (2 * colour + turn + 2 * odd) % 4


def view_swap(array, colour, turn):
    pairs = []
    for view in range(16):
        y, x = view // 4, view % 4
        for brick in range(8):
            dim = link_of(colour, turn, brick % 2)
            flip = 1 if dim < 2 else 3
            other = y * 4 + (x ^ flip) if dim % 2 == 0 else (y ^ flip) * 4 + x
            pairs.append((brick * 16 + view, brick * 16 + other))
    return lax.ppermute(array, ("brick", "view"), pairs)


def make_info(brick, rank):
    view = lax.axis_index("view")
    y = jnp.right_shift(view, 2)
    x = jnp.bitwise_and(view, 3)
    bits = [
        jnp.bitwise_and(x ^ (x >> 1), 1),
        jnp.bitwise_and(y ^ (y >> 1), 1),
        x >> 1,
        y >> 1,
    ]
    odd = jnp.bitwise_and(brick, 1) == 1
    values = [brick, rank]
    for turn in range(2):
        for colour in range(4):
            even_bit, odd_bit = (bits[link_of(colour, turn, at)] for at in range(2))
            values.append(jnp.where(odd, odd_bit, even_bit))
    return jnp.stack(values).astype(jnp.int32)


def work(
    latent_grid, layer_one, layer_two, layer_three, layer_four, view_order, samples, pixel_grad
):
    brick = lax.axis_index("brick")
    info = make_info(brick, jnp.bitwise_xor(brick, view_order[0]))
    voxels = latent_grid.shape[2]

    latent, index, *layers = run_prepare(
        *[
            pltpu.with_memory_space_constraint(array, pltpu.HBM)
            for array in (
                latent_grid[0], samples[0, 0], layer_one.T, layer_two, layer_three, layer_four,
            )
        ]
    )
    plain, turned = layers[:4], layers[4:]

    near = pixel_grad
    for flip in (1, 2):
        near = jnp.concatenate([near, swap_brick(near, flip)], axis=0)
    part_near, trans_near, *saved_near = run_forward(0, info, latent, index, *plain)
    far = swap_brick(near, 6)
    part_far, trans_far, *saved_far = run_forward(4, info, latent, index, *plain)

    own = run_dots(near, far, part_near, part_far, trans_near, trans_far)
    own, state = run_merge(0, 1, info, own, swap_brick(own, 1))
    own, state = run_merge(1, 2, info, own, swap_brick(own, 2), state)
    front, behind, image_near, image_far = run_merge(
        2, 4, info, own, swap_brick(own, 6), state, part_near, part_far
    )

    image = image_near + swap_brick(image_far, 6)
    image = image[:2] + swap_brick(image[2:], 2)
    image = image[:1] + swap_brick(image[1:], 1)

    packed = jnp.zeros((1, 32, TILE), F32)
    grids = []
    for colour in range(4):
        given, saved = (near, saved_near) if colour < 2 else (far, saved_far)
        grid, packed = run_backward(
            2 * colour, info, index, given, front, behind, saved, turned, packed
        )
        grids.append(grid.reshape((2, 2, 4) + grid.shape[2:]))
    for flip in (1, 2, 6):
        packed = packed + swap_brick(packed, flip)
    packed = jnp.concatenate([packed[0, :, k * LANES : (k + 1) * LANES] for k in range(4)], axis=0)
    packed = packed[:104]

    sources = []
    for colour in range(4):
        part = grids[colour]
        for turn in range(2):
            part = part[0] + view_swap(part[1], colour, turn)
        part = part.reshape(-1, LANES)
        rows = part.shape[0]
        if colour == 3:
            part = jnp.concatenate([part, packed], axis=0)
        for turn in (2, 3):
            part = part + view_swap(part, colour, turn)
        got = view_swap(part, colour, 1)
        sent = jnp.concatenate([part[:rows], got[:rows]], axis=0)
        if colour == 3:
            packed = part[rows:] + got[rows:]
            sent = jnp.concatenate([sent, packed], axis=0)
        sources += [part, got, view_swap(sent, colour, 0)]

    channels = latent_grid.shape[1]
    grid, one_t, two, three, four = run_finish(info, sources, packed, channels, voxels)
    return (image, grid, one_t.T, two, three, four)


def solution(mesh):
    in_specs = (
        P("brick", None, None),
        P(),
        P(),
        P(),
        P(),
        P("view"),
        P("view", "brick", None, None),
        P("view", None, "brick"),
    )
    out_specs = (P("view", None, "brick"), P("brick", None, None), P(), P(), P(), P())
    return jax.shard_map(work, mesh=mesh, in_specs=in_specs, out_specs=out_specs, check_vma=False)
```

profile of v0, /device:TPU:0, one launch (start us, length us, event | category | flops | bytes accessed | tf_op | source)
XLA Modules:
  0.0 118.3 jit_solution(11788122721621567449)
XLA Ops:
  3.0 2.1 %collective-permute-start.1 = (f32[2,32,512]{2,1,0:T(8,128)S(1)}, f32[2,32,512]{2,1,0:T(8,128)S(1)}, u32[]{:S(2)}, u32[]{:S(2)}) collective-permute-start(f32[2,32,512]{2,1,0:T(8,128)S(1)} %pad_maximum_fusion.7), channel_id=1, source_target_pairs={{0,32},{16,48},{32,0},{48,16},{64,96},{80,112},{96,64},{112,80},{1... | collective-permute-start | bytes 393224 | tf_op jit(solution)/shard_map/ppermute | solution.py:464
  6.0 3.0 %collective-permute-done.1 = f32[2,32,512]{2,1,0:T(8,128)S(1)} collective-permute-done((f32[2,32,512]{2,1,0:T(8,128)S(1)}, f32[2,32,512]{2,1,0:T(8,128)S(1)}, u32[]{:S(2)}, u32[]{:S(2)}) %collective-permute-start.1) | collective-permute-done | bytes 131104 | tf_op jit(solution)/shard_map/ppermute | solution.py:464
  9.0 3.9 %collective-permute-start.2 = (f32[4,32,512]{2,1,0:T(8,128)S(1)}, f32[4,32,512]{2,1,0:T(8,128)S(1)}, u32[]{:S(2)}, u32[]{:S(2)}) collective-permute-start(f32[4,32,512]{2,1,0:T(8,128)S(1)} %constant_dynamic-update-slice_fusion.near_ref.given_ref), channel_id=1, source_target_pairs={{0,96},{16,112},{32,64},{48,80},{64,32},{80,48},{96,0},{112,16},{1... | collective-permute-start | bytes 786440 | tf_op jit(solution)/shard_map/ppermute | solution.py:464
  15.2 6.9 %forward.2 = (f32[4,32,512]{2,1,0:T(8,128)S(1)}, f32[4,512]{1,0:T(4,128)S(1)}, bf16[4,6,64,4096]{3,2,1,0:T(8,128)(2,1)S(1)}, bf16[4,16,4096]{2,1,0:T(8,128)(2,1)...) custom-call(s32[10]{0:T(128)S(1)} %stack.31.brick_ref.info_ref, ...), custom_call_target="tpu_custom_call" | custom-call | flops 1000000000 | bytes 16000000 | tf_op jit(solution)/shard_map/forward/pallas_call | solution.py:358
  22.1 6.9 %forward.3 = (f32[4,32,512]{2,1,0:T(8,128)S(1)}, f32[4,512]{1,0:T(4,128)S(1)}, bf16[4,6,64,4096]{3,2,1,0:T(8,128)(2,1)S(1)}, bf16[4,16,4096]{2,1,0:T(8,128)(2,1)...) custom-call(s32[10]{0:T(128)S(1)} %stack.31.brick_ref.info_ref, ...), custom_call_target="tpu_custom_call" | custom-call | flops 1000000000 | bytes 16000000 | tf_op jit(solution)/shard_map/forward/pallas_call | solution.py:358
  31.1 3.9 %collective-permute-done.4.got_ref = f32[2,8,512]{2,1,0:T(8,128)S(1)} collective-permute-done((f32[2,8,512]{2,1,0:T(8,128)S(1)}, f32[2,8,512]{2,1,0:T(8,128)S(1)}, u32[]{:S(2)}, u32[]{:S(2)}) %collective-permute-start.4) | collective-permute-done | bytes 32800 | tf_op jit(solution)/shard_map/ppermute | solution.py:464
  35.7 5.1 %collective-permute-done.5.got_ref = f32[2,8,512]{2,1,0:T(8,128)S(1)} collective-permute-done((f32[2,8,512]{2,1,0:T(8,128)S(1)}, f32[2,8,512]{2,1,0:T(8,128)S(1)}, u32[]{:S(2)}, u32[]{:S(2)}) %collective-permute-start.5) | collective-permute-done | bytes 32800 | tf_op jit(solution)/shard_map/ppermute | solution.py:464
  41.5 3.9 %backward.4 = (f32[2,8,64,128]{3,2,1,0:T(8,128)S(1)}, f32[1,32,512]{2,1,0:T(8,128)S(1)}) custom-call(s32[10]{0:T(128)S(1)} %stack.31.brick_ref.info_ref, s32[8,4096]{1,0:T(8,128)S(1)} %get-tuple-element.50.samples_ref, f32[4,32,512]{2,1,0:T(8,128)S(1)} %constant_dynamic-update-slice_fusion.near_ref.given_ref, f32[8,512]{1,0:T(8,128)S(1)} %get-tuple-element.65.weight_ref, ...), custom_call_target="tpu_custom_call" | custom-call | flops 1000000000 | bytes 9000000 | tf_op jit(solution)/shard_map/backward/pallas_call | solution.py:402
  47.1 3.9 %backward.5 = (f32[2,8,64,128]{3,2,1,0:T(8,128)S(1)}, f32[1,32,512]{2,1,0:T(8,128)S(1)}) custom-call(s32[10]{0:T(128)S(1)} %stack.31.brick_ref.info_ref, s32[8,4096]{1,0:T(8,128)S(1)} %get-tuple-element.50.samples_ref, f32[4,32,512]{2,1,0:T(8,128)S(1)} %constant_dynamic-update-slice_fusion.near_ref.given_ref, f32[8,512]{1,0:T(8,128)S(1)} %get-tuple-element.65.weight_ref, ...), custom_call_target="tpu_custom_call" | custom-call | flops 1000000000 | bytes 9000000 | tf_op jit(solution)/shard_map/backward/pallas_call | solution.py:402
  51.0 3.9 %backward.6 = (f32[2,8,64,128]{3,2,1,0:T(8,128)S(1)}, f32[1,32,512]{2,1,0:T(8,128)S(1)}) custom-call(s32[10]{0:T(128)S(1)} %stack.31.brick_ref.info_ref, s32[8,4096]{1,0:T(8,128)S(1)} %get-tuple-element.50.samples_ref, f32[4,32,512]{2,1,0:T(8,128)S(1)} %collective-permute-done.2.far_ref.given_ref, f32[8,512]{1,0:T(8,128)S(1)} %get-tuple-element.65.weight_ref, ...), custom_call_target="tpu_custom_call" | custom-call | flops 1000000000 | bytes 9000000 | tf_op jit(solution)/shard_map/backward/pallas_call | solution.py:402
  55.0 4.0 %backward.7 = (f32[2,8,64,128]{3,2,1,0:T(8,128)S(1)}, f32[1,32,512]{2,1,0:T(8,128)S(1)}) custom-call(s32[10]{0:T(128)S(1)} %stack.31.brick_ref.info_ref, s32[8,4096]{1,0:T(8,128)S(1)} %get-tuple-element.50.samples_ref, f32[4,32,512]{2,1,0:T(8,128)S(1)} %collective-permute-done.2.far_ref.given_ref, f32[8,512]{1,0:T(8,128)S(1)} %get-tuple-element.65.weight_ref, ...), custom_call_target="tpu_custom_call" | custom-call | flops 1000000000 | bytes 9000000 | tf_op jit(solution)/shard_map/backward/pallas_call | solution.py:402
  59.1 2.2 %collective-permute-start.15 = (f32[2,4,64,128]{3,2,1,0:T(8,128)S(1)}, f32[2,4,64,128]{3,2,1,0:T(8,128)S(1)}, u32[]{:S(2)}, u32[]{:S(2)}) collective-permute-start(f32[2,4,64,128]{3,2,1,0:T(8,128)S(1)} %bitcast.69), channel_id=1, source_target_pairs={{0,3},{16,17},{32,35},{48,49},{64,67},{80,81},{96,99},{112,113},{1... | collective-permute-start | bytes 786440 | tf_op jit(solution)/shard_map/ppermute | solution.py:480
  62.3 3.5 %collective-permute-done.30 = f32[1,32,512]{2,1,0:T(8,128)S(1)} collective-permute-done((f32[1,32,512]{2,1,0:T(8,128)S(1)}, f32[1,32,512]{2,1,0:T(8,128)S(1)}, u32[]{:S(2)}, u32[]{:S(2)}) %collective-permute-start.30) | collective-permute-done | bytes 65568 | tf_op jit(solution)/shard_map/ppermute | solution.py:464
  65.8 3.3 %collective-permute-start.31 = (f32[1,32,512]{2,1,0:T(8,128)S(1)}, f32[1,32,512]{2,1,0:T(8,128)S(1)}, u32[]{:S(2)}, u32[]{:S(2)}) collective-permute-start(f32[1,32,512]{2,1,0:T(8,128)S(1)} %add.87), channel_id=1, source_target_pairs={{0,96},{16,112},{32,64},{48,80},{64,32},{80,48},{96,0},{112,16},{1... | collective-permute-start | bytes 196616 | tf_op jit(solution)/shard_map/ppermute | solution.py:464
  69.1 2.2 %collective-permute-done.31 = f32[1,32,512]{2,1,0:T(8,128)S(1)} collective-permute-done((f32[1,32,512]{2,1,0:T(8,128)S(1)}, f32[1,32,512]{2,1,0:T(8,128)S(1)}, u32[]{:S(2)}, u32[]{:S(2)}) %collective-permute-start.31) | collective-permute-done | bytes 65568 | tf_op jit(solution)/shard_map/ppermute | solution.py:464
  74.5 2.3 %collective-permute-start.16 = (f32[4,64,128]{2,1,0:T(8,128)S(1)}, f32[4,64,128]{2,1,0:T(8,128)S(1)}, u32[]{:S(2)}, u32[]{:S(2)}) collective-permute-start(f32[4,64,128]{2,1,0:T(8,128)S(1)} %slice_bitcast_fusion.4), channel_id=1, source_target_pairs={{0,12},{16,20},{32,44},{48,52},{64,76},{80,84},{96,108},{112,116},... | collective-permute-start | bytes 393224 | tf_op jit(solution)/shard_map/ppermute | solution.py:480
  79.0 3.1 %collective-permute-start.28 = (f32[4,64,128]{2,1,0:T(8,128)S(1)}, f32[4,64,128]{2,1,0:T(8,128)S(1)}, u32[]{:S(2)}, u32[]{:S(2)}) collective-permute-start(f32[4,64,128]{2,1,0:T(8,128)S(1)} %slice_bitcast_fusion), channel_id=1, source_target_pairs={{0,12},{16,20},{32,44},{48,52},{64,76},{80,84},{96,108},{112,116},... | collective-permute-start | bytes 393224 | tf_op jit(solution)/shard_map/ppermute | solution.py:480
  83.5 2.2 %collective-permute-start.23 = (f32[256,128]{1,0:T(8,128)S(1)}, f32[256,128]{1,0:T(8,128)S(1)}, u32[]{:S(2)}, u32[]{:S(2)}) collective-permute-start(f32[256,128]{1,0:T(8,128)S(1)} %bitcast.66), channel_id=1, source_target_pairs={{0,3},{16,17},{32,35},{48,49},{64,67},{80,81},{96,99},{112,113},{1... | collective-permute-start | bytes 393224 | tf_op jit(solution)/shard_map/ppermute | solution.py:480
  93.5 1.9 %collective-permute-done.12 = f32[256,128]{1,0:T(8,128)S(1)} collective-permute-done((f32[256,128]{1,0:T(8,128)S(1)}, f32[256,128]{1,0:T(8,128)S(1)}, u32[]{:S(2)}, u32[]{:S(2)}) %collective-permute-start.12) | collective-permute-done | bytes 131104 | tf_op jit(solution)/shard_map/ppermute | solution.py:480
  95.8 2.1 %collective-permute-start.19 = (f32[256,128]{1,0:T(8,128)S(1)}, f32[256,128]{1,0:T(8,128)S(1)}, u32[]{:S(2)}, u32[]{:S(2)}) collective-permute-start(f32[256,128]{1,0:T(8,128)S(1)} %add.79.refs_3_), channel_id=1, source_target_pairs={{0,12},{16,20},{32,44},{48,52},{64,76},{80,84},{96,108},{112,116},... | collective-permute-start | bytes 393224 | tf_op jit(solution)/shard_map/ppermute | solution.py:480
  102.1 2.4 %collective-permute-start.20 = (f32[512,128]{1,0:T(8,128)S(1)}, f32[512,128]{1,0:T(8,128)S(1)}, u32[]{:S(2)}, u32[]{:S(2)}) collective-permute-start(f32[512,128]{1,0:T(8,128)S(1)} %pad_maximum_fusion.2), channel_id=1, source_target_pairs={{0,3},{16,17},{32,35},{48,49},{64,67},{80,81},{96,99},{112,113},{1... | collective-permute-start | bytes 786440 | tf_op jit(solution)/shard_map/ppermute | solution.py:480
  104.6 1.8 %collective-permute-done.34.refs_10_ = f32[360,128]{1,0:T(8,128)S(1)} collective-permute-done((f32[360,128]{1,0:T(8,128)S(1)}, f32[360,128]{1,0:T(8,128)S(1)}, u32[]{:S(2)}, u32[]{:S(2)}) %collective-permute-start.34) | collective-permute-done | bytes 184352 | tf_op jit(solution)/shard_map/ppermute | solution.py:480
  110.3 5.8 %collective-permute-done.26.refs_8_ = f32[512,128]{1,0:T(8,128)S(1)} collective-permute-done((f32[512,128]{1,0:T(8,128)S(1)}, f32[512,128]{1,0:T(8,128)S(1)}, u32[]{:S(2)}, u32[]{:S(2)}) %collective-permute-start.26) | collective-permute-done | bytes 262176 | tf_op jit(solution)/shard_map/ppermute | solution.py:480
  116.1 2.2 %finish.1 = (f32[1,16,32768]{2,1,0:T(8,128)}, f32[16,64]{1,0:T(8,128)}, f32[64,64]{1,0:T(8,128)}, f32[64,64]{1,0:T(8,128)}, f32[33,64]{1,0:T(8,128)}) custom-call(s32[10]{0:T(128)S(1)} %stack.31.brick_ref.info_ref, f32[256,128]{1,0:T(8,128)S(1)} %add.75.refs_0_, f32[256,128]{1,0:T(8,128)S(1)} %collective-permute-done.13.refs_1_, ...), custom_call_target="tpu_custom_call" | custom-call | tf_op jit(solution)/shard_map/finish/pallas_call | solution.py:447
  (107 shorter events, 33.9 us)
Async XLA Ops:
  9.0 20.1 %collective-permute-start.2 = (f32[4,32,512]{2,1,0:T(8,128)S(1)}, f32[4,32,512]{2,1,0:T(8,128)S(1)}, u32[]{:S(2)}, u32[]{:S(2)}) collective-permute-start(f32[4,32,512]{2,1,0:T(8,128)S(1)} %constant_dynamic-update-slice_fusion.near_ref.given_ref), channel_id=1, source_target_pairs={{0,96},{16,112},{32,64},{48,80},{64,32},{80,48},{96,0},{112,16},{1... | collective-permute-start | bytes 786440 | tf_op jit(solution)/shard_map/ppermute | solution.py:464
  41.4 31.2 %collective-permute-start.6 = (f32[4,32,512]{2,1,0:T(8,128)S(1)}, f32[4,32,512]{2,1,0:T(8,128)S(1)}, u32[]{:S(2)}, u32[]{:S(2)}) collective-permute-start(f32[4,32,512]{2,1,0:T(8,128)S(1)} %get-tuple-element.64), channel_id=1, source_target_pairs={{0,96},{16,112},{32,64},{48,80},{64,32},{80,48},{96,0},{112,16},{1... | collective-permute-start | bytes 786440 | tf_op jit(solution)/shard_map/ppermute | solution.py:464
  45.5 27.2 %collective-permute-start.9 = (f32[2,4,64,128]{3,2,1,0:T(8,128)S(1)}, f32[2,4,64,128]{3,2,1,0:T(8,128)S(1)}, u32[]{:S(2)}, u32[]{:S(2)}) collective-permute-start(f32[2,4,64,128]{3,2,1,0:T(8,128)S(1)} %bitcast.68), channel_id=1, source_target_pairs={{0,1},{16,19},{32,33},{48,51},{64,65},{80,83},{96,97},{112,115},{1... | collective-permute-start | bytes 786440 | tf_op jit(solution)/shard_map/ppermute | solution.py:480
  59.1 15.4 %collective-permute-start.15 = (f32[2,4,64,128]{3,2,1,0:T(8,128)S(1)}, f32[2,4,64,128]{3,2,1,0:T(8,128)S(1)}, u32[]{:S(2)}, u32[]{:S(2)}) collective-permute-start(f32[2,4,64,128]{3,2,1,0:T(8,128)S(1)} %bitcast.69), channel_id=1, source_target_pairs={{0,3},{16,17},{32,35},{48,49},{64,67},{80,81},{96,99},{112,113},{1... | collective-permute-start | bytes 786440 | tf_op jit(solution)/shard_map/ppermute | solution.py:480
  61.6 15.2 %collective-permute-start.21 = (f32[2,4,64,128]{3,2,1,0:T(8,128)S(1)}, f32[2,4,64,128]{3,2,1,0:T(8,128)S(1)}, u32[]{:S(2)}, u32[]{:S(2)}) collective-permute-start(f32[2,4,64,128]{3,2,1,0:T(8,128)S(1)} %bitcast.70), channel_id=1, source_target_pairs={{0,1},{16,19},{32,33},{48,51},{64,65},{80,83},{96,97},{112,115},{1... | collective-permute-start | bytes 786440 | tf_op jit(solution)/shard_map/ppermute | solution.py:480
  71.4 7.6 %collective-permute-start.27 = (f32[2,4,64,128]{3,2,1,0:T(8,128)S(1)}, f32[2,4,64,128]{3,2,1,0:T(8,128)S(1)}, u32[]{:S(2)}, u32[]{:S(2)}) collective-permute-start(f32[2,4,64,128]{3,2,1,0:T(8,128)S(1)} %bitcast.71), channel_id=1, source_target_pairs={{0,3},{16,17},{32,35},{48,49},{64,67},{80,81},{96,99},{112,113},{1... | collective-permute-start | bytes 786440 | tf_op jit(solution)/shard_map/ppermute | solution.py:480
  72.6 25.3 %collective-permute-start.7 = (f32[2,32,512]{2,1,0:T(8,128)S(1)}, f32[2,32,512]{2,1,0:T(8,128)S(1)}, u32[]{:S(2)}, u32[]{:S(2)}) collective-permute-start(f32[2,32,512]{2,1,0:T(8,128)S(1)} %slice.125), channel_id=1, source_target_pairs={{0,32},{16,48},{32,0},{48,16},{64,96},{80,112},{96,64},{112,80},{1... | collective-permute-start | bytes 393224 | tf_op jit(solution)/shard_map/ppermute | solution.py:464
  72.8 9.3 %collective-permute-start.10 = (f32[4,64,128]{2,1,0:T(8,128)S(1)}, f32[4,64,128]{2,1,0:T(8,128)S(1)}, u32[]{:S(2)}, u32[]{:S(2)}) collective-permute-start(f32[4,64,128]{2,1,0:T(8,128)S(1)} %slice_bitcast_fusion.6), channel_id=1, source_target_pairs={{0,4},{16,28},{32,36},{48,60},{64,68},{80,92},{96,100},{112,124},{... | collective-permute-start | bytes 393224 | tf_op jit(solution)/shard_map/ppermute | solution.py:480
  74.5 8.9 %collective-permute-start.16 = (f32[4,64,128]{2,1,0:T(8,128)S(1)}, f32[4,64,128]{2,1,0:T(8,128)S(1)}, u32[]{:S(2)}, u32[]{:S(2)}) collective-permute-start(f32[4,64,128]{2,1,0:T(8,128)S(1)} %slice_bitcast_fusion.4), channel_id=1, source_target_pairs={{0,12},{16,20},{32,44},{48,52},{64,76},{80,84},{96,108},{112,116},... | collective-permute-start | bytes 393224 | tf_op jit(solution)/shard_map/ppermute | solution.py:480
  76.8 6.7 %collective-permute-start.22 = (f32[4,64,128]{2,1,0:T(8,128)S(1)}, f32[4,64,128]{2,1,0:T(8,128)S(1)}, u32[]{:S(2)}, u32[]{:S(2)}) collective-permute-start(f32[4,64,128]{2,1,0:T(8,128)S(1)} %slice_bitcast_fusion.2), channel_id=1, source_target_pairs={{0,4},{16,28},{32,36},{48,60},{64,68},{80,92},{96,100},{112,124},{... | collective-permute-start | bytes 393224 | tf_op jit(solution)/shard_map/ppermute | solution.py:480
  79.0 6.7 %collective-permute-start.28 = (f32[4,64,128]{2,1,0:T(8,128)S(1)}, f32[4,64,128]{2,1,0:T(8,128)S(1)}, u32[]{:S(2)}, u32[]{:S(2)}) collective-permute-start(f32[4,64,128]{2,1,0:T(8,128)S(1)} %slice_bitcast_fusion), channel_id=1, source_target_pairs={{0,12},{16,20},{32,44},{48,52},{64,76},{80,84},{96,108},{112,116},... | collective-permute-start | bytes 393224 | tf_op jit(solution)/shard_map/ppermute | solution.py:480
  82.1 6.3 %collective-permute-start.11 = (f32[256,128]{1,0:T(8,128)S(1)}, f32[256,128]{1,0:T(8,128)S(1)}, u32[]{:S(2)}, u32[]{:S(2)}) collective-permute-start(f32[256,128]{1,0:T(8,128)S(1)} %bitcast.64), channel_id=1, source_target_pairs={{0,3},{16,17},{32,35},{48,49},{64,67},{80,81},{96,99},{112,113},{1... | collective-permute-start | bytes 393224 | tf_op jit(solution)/shard_map/ppermute | solution.py:480
  83.4 6.7 %collective-permute-start.17 = (f32[256,128]{1,0:T(8,128)S(1)}, f32[256,128]{1,0:T(8,128)S(1)}, u32[]{:S(2)}, u32[]{:S(2)}) collective-permute-start(f32[256,128]{1,0:T(8,128)S(1)} %bitcast.65), channel_id=1, source_target_pairs={{0,1},{16,19},{32,33},{48,51},{64,65},{80,83},{96,97},{112,115},{1... | collective-permute-start | bytes 393224 | tf_op jit(solution)/shard_map/ppermute | solution.py:480
  83.5 7.0 %collective-permute-start.23 = (f32[256,128]{1,0:T(8,128)S(1)}, f32[256,128]{1,0:T(8,128)S(1)}, u32[]{:S(2)}, u32[]{:S(2)}) collective-permute-start(f32[256,128]{1,0:T(8,128)S(1)} %bitcast.66), channel_id=1, source_target_pairs={{0,3},{16,17},{32,35},{48,49},{64,67},{80,81},{96,99},{112,113},{1... | collective-permute-start | bytes 393224 | tf_op jit(solution)/shard_map/ppermute | solution.py:480
  88.4 6.9 %collective-permute-start.12 = (f32[256,128]{1,0:T(8,128)S(1)}, f32[256,128]{1,0:T(8,128)S(1)}, u32[]{:S(2)}, u32[]{:S(2)}) collective-permute-start(f32[256,128]{1,0:T(8,128)S(1)} %bitcast_add_fusion.2), channel_id=1, source_target_pairs={{0,12},{16,20},{32,44},{48,52},{64,76},{80,84},{96,108},{112,116},... | collective-permute-start | bytes 393224 | tf_op jit(solution)/shard_map/ppermute | solution.py:480
  90.5 7.5 %collective-permute-start.24 = (f32[256,128]{1,0:T(8,128)S(1)}, f32[256,128]{1,0:T(8,128)S(1)}, u32[]{:S(2)}, u32[]{:S(2)}) collective-permute-start(f32[256,128]{1,0:T(8,128)S(1)} %bitcast_add_fusion), channel_id=1, source_target_pairs={{0,12},{16,20},{32,44},{48,52},{64,76},{80,84},{96,108},{112,116},... | collective-permute-start | bytes 393224 | tf_op jit(solution)/shard_map/ppermute | solution.py:480
  92.0 7.6 %collective-permute-start.33 = (f32[360,128]{1,0:T(8,128)S(1)}, f32[360,128]{1,0:T(8,128)S(1)}, u32[]{:S(2)}, u32[]{:S(2)}) collective-permute-start(f32[360,128]{1,0:T(8,128)S(1)} %add.89), channel_id=1, source_target_pairs={{0,4},{16,28},{32,36},{48,60},{64,68},{80,92},{96,100},{112,124},{... | collective-permute-start | bytes 552968 | tf_op jit(solution)/shard_map/ppermute | solution.py:480
  97.9 9.7 %collective-permute-start.8 = (f32[1,32,512]{2,1,0:T(8,128)S(1)}, f32[1,32,512]{2,1,0:T(8,128)S(1)}, u32[]{:S(2)}, u32[]{:S(2)}) collective-permute-start(f32[1,32,512]{2,1,0:T(8,128)S(1)} %slice.127), channel_id=1, source_target_pairs={{0,16},{16,0},{32,48},{48,32},{64,80},{80,64},{96,112},{112,96},{1... | collective-permute-start | bytes 196616 | tf_op jit(solution)/shard_map/ppermute | solution.py:464
  98.1 9.4 %collective-permute-start.25 = (f32[256,128]{1,0:T(8,128)S(1)}, f32[256,128]{1,0:T(8,128)S(1)}, u32[]{:S(2)}, u32[]{:S(2)}) collective-permute-start(f32[256,128]{1,0:T(8,128)S(1)} %add.83.refs_6_), channel_id=1, source_target_pairs={{0,4},{16,28},{32,36},{48,60},{64,68},{80,92},{96,100},{112,124},{... | collective-permute-start | bytes 393224 | tf_op jit(solution)/shard_map/ppermute | solution.py:480
  99.6 6.8 %collective-permute-start.34 = (f32[360,128]{1,0:T(8,128)S(1)}, f32[360,128]{1,0:T(8,128)S(1)}, u32[]{:S(2)}, u32[]{:S(2)}) collective-permute-start(f32[360,128]{1,0:T(8,128)S(1)} %add.90.refs_9_), channel_id=1, source_target_pairs={{0,12},{16,20},{32,44},{48,52},{64,76},{80,84},{96,108},{112,116},... | collective-permute-start | bytes 552968 | tf_op jit(solution)/shard_map/ppermute | solution.py:480
  100.8 9.3 %collective-permute-start.14 = (f32[512,128]{1,0:T(8,128)S(1)}, f32[512,128]{1,0:T(8,128)S(1)}, u32[]{:S(2)}, u32[]{:S(2)}) collective-permute-start(f32[512,128]{1,0:T(8,128)S(1)} %pad_maximum_fusion.1), channel_id=1, source_target_pairs={{0,1},{16,19},{32,33},{48,51},{64,65},{80,83},{96,97},{112,115},{1... | collective-permute-start | bytes 786440 | tf_op jit(solution)/shard_map/ppermute | solution.py:480
  102.1 8.2 %collective-permute-start.20 = (f32[512,128]{1,0:T(8,128)S(1)}, f32[512,128]{1,0:T(8,128)S(1)}, u32[]{:S(2)}, u32[]{:S(2)}) collective-permute-start(f32[512,128]{1,0:T(8,128)S(1)} %pad_maximum_fusion.2), channel_id=1, source_target_pairs={{0,3},{16,17},{32,35},{48,49},{64,67},{80,81},{96,99},{112,113},{1... | collective-permute-start | bytes 786440 | tf_op jit(solution)/shard_map/ppermute | solution.py:480
  106.5 9.6 %collective-permute-start.35 = (f32[616,128]{1,0:T(8,128)S(1)}, f32[616,128]{1,0:T(8,128)S(1)}, u32[]{:S(2)}, u32[]{:S(2)}) collective-permute-start(f32[616,128]{1,0:T(8,128)S(1)} %pad_maximum_fusion), channel_id=1, source_target_pairs={{0,3},{16,17},{32,35},{48,49},{64,67},{80,81},{96,99},{112,113},{1... | collective-permute-start | bytes 946184 | tf_op jit(solution)/shard_map/ppermute | solution.py:480
  107.5 8.6 %collective-permute-start.26 = (f32[512,128]{1,0:T(8,128)S(1)}, f32[512,128]{1,0:T(8,128)S(1)}, u32[]{:S(2)}, u32[]{:S(2)}) collective-permute-start(f32[512,128]{1,0:T(8,128)S(1)} %pad_maximum_fusion.3), channel_id=1, source_target_pairs={{0,1},{16,19},{32,33},{48,51},{64,65},{80,83},{96,97},{112,115},{1... | collective-permute-start | bytes 786440 | tf_op jit(solution)/shard_map/ppermute | solution.py:480
  (12 other events, 53.9 us)
where the time goes:
time: 119 us; the launch traced here: 118 us
  starting transfers between devices  42 us (35%)
  waiting for transfers between devices  36.2 us (30%)
  Pallas kernels  35.1 us (29%)
  other arithmetic  2.04 us (2%)
  between operations  1.73 us (1%)
  local copies, waits for them, and re-layouts  1.19 us (1%)
    ppermute x24, starting transfers between devices, view_swap(): return lax.ppermute(array, ('brick', 'view'), pairs)  31.7 us
    ppermute x12, waiting for transfers between devices, swap_brick(): return lax.ppermute(array, 'brick', [(i, i ^ flip) for i in range(8)])  20.4 us
    ppermute x24, waiting for transfers between devices, view_swap(): return lax.ppermute(array, ('brick', 'view'), pairs)  15.8 us
    pallas_call x4, Pallas kernels, run_backward(): pl.pallas_call(functools.partial(backward_kernel, first), out_shape=[jax....  15.8 us
    pallas_call x2, Pallas kernels, run_forward(): pl.pallas_call(functools.partial(forward_kernel, first), out_shape=shapes...  13.9 us
    ppermute x12, starting transfers between devices, swap_brick(): return lax.ppermute(array, 'brick', [(i, i ^ flip) for i in range(8)])  10.3 us
  transfers between devices with their start and end apart: 36, of which 16 were waited for; matrix products, arithmetic and copies ran while one was open for 2% of the time, Pallas kernels for 26%

commit v1 on v0

--- a/solution.py
+++ b/solution.py
@@ -16,6 +16,11 @@
 LANES = 128
 PARTS = TILE // LANES
 OUT_ROWS = 40
+SIZES = (3, 3, 2)
+FIRSTS = tuple(sum(SIZES[:c]) for c in range(len(SIZES)))
+COLOURS = len(SIZES)
+LAST = COLOURS - 1
+SPLIT = 6
 
 
 def mm(a, b):
@@ -32,8 +37,9 @@
 
 def one_hot(local):
     low = jnp.bitwise_and(local, LANES - 1)
-    rows = lax.broadcasted_iota(jnp.int32, (LANES, local.shape[1]), 0)
-    return jnp.where(rows == low, 1.0, 0.0).astype(BF16)
+    rows = lax.broadcasted_iota(jnp.int16, (LANES, local.shape[1]), 0)
+    match = rows == jnp.broadcast_to(low.astype(jnp.int16), rows.shape)
+    return jnp.where(match, jnp.ones(rows.shape, BF16), jnp.zeros(rows.shape, BF16))
 
 
 def row_of(array, step):
@@ -105,16 +111,16 @@
 
 
 def backward_kernel(
-    first, brick_ref, samples_ref, given_ref, weight_ref, behind_ref, hidden_ref, feature_ref,
+    colour, brick_ref, samples_ref, near_ref, far_ref, weight_ref, behind_ref, hidden_ref, feature_ref,
     colour_ref, ray_ref, one_t_ref, two_t_ref, three_t_ref, four_t_ref, before_ref,
     grid_ref, packed_ref, cot_ref, out_ref, feature_cot_ref,
 ):
-    place = pl.program_id(0) + first
+    place = pl.program_id(0) + FIRSTS[colour]
     channels = feature_ref.shape[1]
 
     @pl.when(pl.program_id(0) == 0)
     def _():
-        if first == 0:
+        if colour == 0:
             packed_ref[...] = jnp.zeros_like(packed_ref)
         else:
             packed_ref[...] = before_ref[...]
@@ -123,7 +129,7 @@
     trans_grad = weight * behind_ref[pl.ds(place, 1), :]
     factor = ray_ref[0, 0]
     through = ray_ref[0, 1]
-    scaled = weight * given_ref[0]
+    scaled = weight * jnp.where(place < 4, near_ref[0], far_ref[0])
     dots = jnp.concatenate(
         [
             jnp.sum(scaled * colour_at(colour_ref, step), axis=0, keepdims=True)
@@ -140,10 +146,10 @@
     first_row = lax.broadcasted_iota(jnp.int32, (OUT_ROWS - 32, TILE), 0) == 0
     for step in range(STEPS):
         span = pl.ds(step * TILE, TILE)
-        colour = colour_at(colour_ref, step)
+        shade = colour_at(colour_ref, step)
         out_ref[:, span] = jnp.concatenate(
             [
-                (colour - colour * colour) * (row_of(factor, step) * scaled),
+                (shade - shade * shade) * (row_of(factor, step) * scaled),
                 jnp.where(first_row, row_of(last, step), 0.0),
             ],
             axis=0,
@@ -174,8 +180,9 @@
         spread = jnp.concatenate(
             [jnp.where(high == k, feature_cot, 0.0) for k in range(PARTS)], axis=0
         ).astype(BF16)
-        half = jnp.bitwise_xor(step // 4, brick_ref[6 + first // 2])
-        grid_ref[0, half * 4 + step % 4] = mm_nt(spread, one_hot(local))
+        half = jnp.bitwise_xor(step // 4, brick_ref[2 + colour])
+        quarter = jnp.bitwise_xor(step // 2 % 2, brick_ref[2 + COLOURS + colour])
+        grid_ref[half, quarter, 0, step % 2] = mm_nt(spread, one_hot(local))
 
     for half in range(2):
         rows = slice(32 * half, 32 * half + 32)
@@ -217,24 +224,21 @@
     return jnp.where(upper, pltpu.roll(array, 8 - flip, 0), pltpu.roll(array, flip, 0))
 
 
-def dots_kernel(near_ref, far_ref, part_near_ref, part_far_ref, trans_near_ref, trans_far_ref, out_ref):
-    out_ref[0, 0:4, :] = trans_near_ref[...]
-    out_ref[0, 4:8, :] = trans_far_ref[...]
-    for half, (given_ref, part_ref) in enumerate(
-        ((near_ref, part_near_ref), (far_ref, part_far_ref))
-    ):
-        for p in range(4):
-            row = 4 * half + p
-            out_ref[1, row : row + 1, :] = jnp.sum(
-                given_ref[p] * part_ref[p], axis=0, keepdims=True
-            )
-
-
-def merge_kernel(level, flip, info_ref, own_ref, got_ref, *refs):
+def dots_kernel(near_ref, far_ref, part_low_ref, part_high_ref, trans_low_ref, trans_high_ref, out_ref):
+    out_ref[0, 0:SPLIT, :] = trans_low_ref[...]
+    out_ref[0, SPLIT:8, :] = trans_high_ref[...]
+    for p in range(8):
+        given = near_ref[p] if p < 4 else far_ref[p - 4]
+        part = part_low_ref[p] if p < SPLIT else part_high_ref[p - SPLIT]
+        out_ref[1, p : p + 1, :] = jnp.sum(given * part, axis=0, keepdims=True)
+
+
+def merge_kernel(level, flip, info_ref, order_ref, own_ref, got_ref, *refs):
     total, dots = own_ref[0], own_ref[1]
     got_total = flip_rows(got_ref[0], flip)
     got_dots = flip_rows(got_ref[1], flip)
-    bit = jnp.bitwise_and(jnp.right_shift(info_ref[1], level), 1)
+    rank = jnp.bitwise_xor(info_ref[0], order_ref[0])
+    bit = jnp.bitwise_and(jnp.right_shift(rank, level), 1)
     first = jnp.full(total.shape, bit, jnp.int32) == 0
     if level == 0:
         front, after, behind = jnp.ones_like(total), jnp.ones_like(total), jnp.zeros_like(total)
@@ -251,35 +255,37 @@
         out_ref[0] = total * got_total
         out_ref[1] = jnp.where(first, dots + total * got_dots, got_dots + got_total * dots)
     else:
-        part_near_ref, part_far_ref, front_ref, behind_ref, image_near_ref, image_far_ref = refs
+        part_low_ref, part_high_ref, front_ref, behind_ref, image_near_ref, image_far_ref = refs
         front_ref[...] = front
         behind_ref[...] = behind
-        for p in range(4):
-            image_near_ref[p] = front[p : p + 1] * part_near_ref[p]
-            image_far_ref[p] = front[p + 4 : p + 5] * part_far_ref[p]
+        for p in range(8):
+            part = part_low_ref[p] if p < SPLIT else part_high_ref[p - SPLIT]
+            image_ref = image_near_ref if p < 4 else image_far_ref
+            image_ref[p % 4] = front[p : p + 1] * part
 
 
 def finish_kernel(info_ref, *refs):
-    sources, (packed_in_ref, grid_ref, one_t_ref, two_ref, three_ref, four_ref) = refs[:12], refs[12:]
+    sources, (packed_in_ref, grid_ref, one_t_ref, two_ref, three_ref, four_ref) = refs[: 3 * COLOURS], refs[3 * COLOURS :]
     channels = grid_ref.shape[1]
     slab = grid_ref.shape[2] // STEPS
 
-    rows = 4 * PARTS * channels
-    for colour in range(4):
-        bit = info_ref[2 + colour]
+    unit = PARTS * channels
+    for colour in range(COLOURS):
+        rows = 2 * SIZES[colour] * unit
         for part in range(4):
             source = sources[3 * colour + min(part, 2)]
             skip = rows if part == 3 else 0
-            tile = place_to_tile(2 * colour + jnp.bitwise_xor(bit, part // 2), info_ref[0])
-            half = jnp.bitwise_xor(info_ref[6 + colour], part % 2)
-            for step in range(4):
-                for k in range(PARTS):
-                    base = (half * 4 + step) * slab + tile * TILE + k * LANES
-                    row = skip + (step * PARTS + k) * channels
-                    grid_ref[0, :, pl.ds(pl.multiple_of(base, LANES), LANES)] = source[
-                        row : row + channels, :
-                    ]
-    packed_in_ref = packed_in_ref[...] + sources[11][2 * rows :, :]
+            half = jnp.bitwise_xor(info_ref[2 + colour], part // 2)
+            quarter = jnp.bitwise_xor(info_ref[2 + COLOURS + colour], part % 2)
+            for at in range(SIZES[colour]):
+                tile = place_to_tile(FIRSTS[colour] + at, info_ref[0])
+                for step in range(2):
+                    start = (half * 4 + quarter * 2 + step) * slab + tile * TILE
+                    for k in range(PARTS):
+                        row = skip + (at * 2 + step) * unit + k * channels
+                        span = pl.ds(pl.multiple_of(start + k * LANES, LANES), LANES)
+                        grid_ref[0, :, span] = source[row : row + channels, :]
+    packed_in_ref = packed_in_ref[...] + sources[3 * LAST + 2][2 * rows :, :]
     one_t_ref[...] = packed_in_ref[64:80, 64:128]
     two_ref[...] = packed_in_ref[0:64, 0:64]
     three_ref[...] = packed_in_ref[0:64, 64:128]
@@ -320,7 +326,7 @@
     )(*arrays)
 
 
-def run_merge(level, flip, info, own, got, *more):
+def run_merge(level, flip, info, order, own, got, *more):
     shapes = {
         False: [(2, 8, TILE), (3, 8, TILE)],
         True: [(8, TILE), (8, TILE), (4, 32, TILE), (4, 32, TILE)],
@@ -328,11 +334,11 @@
     return pl.pallas_call(
         functools.partial(merge_kernel, level, flip),
         out_shape=[jax.ShapeDtypeStruct(shape, F32) for shape in shapes],
-        in_specs=[SMEM] + [VMEM] * (2 + len(more)),
+        in_specs=[SMEM, SMEM] + [VMEM] * (2 + len(more)),
         out_specs=[VMEM] * len(shapes),
         compiler_params=SMALL,
         name="merge",
-    )(info, own, got, *more)
+    )(info, order, own, got, *more)
 
 
 def whole(shape):
@@ -343,8 +349,7 @@
     return pl.BlockSpec((1,) + shape, lambda p, brick: (p,) + (0,) * len(shape))
 
 
-def run_forward(first, brick, grid, samples, one, two, three, four):
-    count = 4
+def run_forward(first, count, brick, grid, samples, one, two, three, four):
     wide = STEPS * TILE
     channels = grid.shape[0]
     shapes = [
@@ -382,27 +387,30 @@
             scratch_shapes=[pltpu.VMEM((STEPS, TILE), F32)],
         ),
         cost_estimate=pl.CostEstimate(
-            flops=1_000_000_000, bytes_accessed=16_000_000, transcendentals=4_000_000
+            flops=250_000_000 * count,
+            bytes_accessed=4_000_000 * count,
+            transcendentals=1_000_000 * count,
         ),
         compiler_params=pltpu.CompilerParams(vmem_limit_bytes=14 * 2**20),
         name="forward",
     )(brick, grid, samples, one, two, three, four)
 
 
-def run_backward(first, brick, samples, given, weight, behind, saved, layers, before):
-    count = 2
-    skip = first % 4
+def run_backward(colour, brick, samples, near, far, weight, behind, saved, layers, before):
+    count = SIZES[colour]
+    first = FIRSTS[colour]
+    skip = first % SPLIT
     wide = STEPS * TILE
-    hidden, feature, colour, ray = saved
+    hidden, feature, shade, ray = saved
     channels = feature.shape[1]
 
     def later(shape):
         return pl.BlockSpec((1,) + shape, lambda p, brick: (p + skip,) + (0,) * len(shape))
 
     return pl.pallas_call(
-        functools.partial(backward_kernel, first),
+        functools.partial(backward_kernel, colour),
         out_shape=[
-            jax.ShapeDtypeStruct((count, STEPS, PARTS * channels, LANES), F32),
+            jax.ShapeDtypeStruct((2, 2, count, 2, PARTS * channels, LANES), F32),
             jax.ShapeDtypeStruct((1, 32, TILE), F32),
         ],
         grid_spec=pltpu.PrefetchScalarGridSpec(
@@ -412,7 +420,8 @@
                 pl.BlockSpec(
                     (STEPS, TILE), lambda p, brick: (0, place_to_tile(p + first, brick[0]))
                 ),
-                later((32, TILE)),
+                pl.BlockSpec((1, 32, TILE), lambda p, brick: (jnp.minimum(p + first, 3), 0, 0)),
+                pl.BlockSpec((1, 32, TILE), lambda p, brick: (jnp.maximum(p + first, 4) - 4, 0, 0)),
                 whole(weight.shape),
                 whole(behind.shape),
                 later((6, 64, wide)),
@@ -424,8 +433,7 @@
             ],
             out_specs=[
                 pl.BlockSpec(
-                    (1, STEPS, PARTS * channels, LANES),
-                    lambda p, brick: (jnp.bitwise_xor(p, brick[2 + first // 2]), 0, 0, 0),
+                    (2, 2, 1, 2, PARTS * channels, LANES), lambda p, brick: (0, 0, p, 0, 0, 0)
                 ),
                 whole((1, 32, TILE)),
             ],
@@ -436,11 +444,13 @@
             ],
         ),
         cost_estimate=pl.CostEstimate(
-            flops=1_000_000_000, bytes_accessed=9_000_000, transcendentals=0
+            flops=500_000_000 * count, bytes_accessed=4_500_000 * count, transcendentals=0
         ),
         compiler_params=pltpu.CompilerParams(vmem_limit_bytes=14 * 2**20),
         name="backward",
-    )(brick, samples, given, weight, behind, hidden, feature, colour, ray, *layers, before)
+    )(
+        brick, samples, near, far, weight, behind, hidden, feature, shade, ray, *layers, before
+    )
 
 
 def run_finish(info, sources, packed, channels, voxels):
@@ -453,7 +463,7 @@
             jax.ShapeDtypeStruct((64, 64), F32),
             jax.ShapeDtypeStruct((33, 64), F32),
         ],
-        in_specs=[SMEM] + [VMEM] * 13,
+        in_specs=[SMEM] + [VMEM] * (3 * COLOURS + 1),
         out_specs=[VMEM] * 5,
         compiler_params=pltpu.CompilerParams(vmem_limit_bytes=14 * 2**20),
         name="finish",
@@ -480,7 +490,7 @@
     return lax.ppermute(array, ("brick", "view"), pairs)
 
 
-def make_info(brick, rank):
+def make_info(brick):
     view = lax.axis_index("view")
     y = jnp.right_shift(view, 2)
     x = jnp.bitwise_and(view, 3)
@@ -491,9 +501,9 @@
         y >> 1,
     ]
     odd = jnp.bitwise_and(brick, 1) == 1
-    values = [brick, rank]
+    values = [brick, brick]
     for turn in range(2):
-        for colour in range(4):
+        for colour in range(COLOURS):
             even_bit, odd_bit = (bits[link_of(colour, turn, at)] for at in range(2))
             values.append(jnp.where(odd, odd_bit, even_bit))
     return jnp.stack(values).astype(jnp.int32)
@@ -503,7 +513,7 @@
     latent_grid, layer_one, layer_two, layer_three, layer_four, view_order, samples, pixel_grad
 ):
     brick = lax.axis_index("brick")
-    info = make_info(brick, jnp.bitwise_xor(brick, view_order[0]))
+    info = make_info(brick)
     voxels = latent_grid.shape[2]
 
     latent, index, *layers = run_prepare(
@@ -516,18 +526,17 @@
     )
     plain, turned = layers[:4], layers[4:]
 
-    near = pixel_grad
-    for flip in (1, 2):
-        near = jnp.concatenate([near, swap_brick(near, flip)], axis=0)
-    part_near, trans_near, *saved_near = run_forward(0, info, latent, index, *plain)
+    near = [pixel_grad] + [swap_brick(pixel_grad, flip) for flip in (1, 2, 3)]
+    part_low, trans_low, *saved_low = run_forward(0, SPLIT, info, latent, index, *plain)
+    near = jnp.concatenate(near, axis=0)
     far = swap_brick(near, 6)
-    part_far, trans_far, *saved_far = run_forward(4, info, latent, index, *plain)
-
-    own = run_dots(near, far, part_near, part_far, trans_near, trans_far)
-    own, state = run_merge(0, 1, info, own, swap_brick(own, 1))
-    own, state = run_merge(1, 2, info, own, swap_brick(own, 2), state)
+    part_high, trans_high, *saved_high = run_forward(SPLIT, 8 - SPLIT, info, latent, index, *plain)
+
+    own = run_dots(near, far, part_low, part_high, trans_low, trans_high)
+    own, state = run_merge(0, 1, info, view_order, own, swap_brick(own, 1))
+    own, state = run_merge(1, 2, info, view_order, own, swap_brick(own, 2), state)
     front, behind, image_near, image_far = run_merge(
-        2, 4, info, own, swap_brick(own, 6), state, part_near, part_far
+        2, 4, info, view_order, own, swap_brick(own, 6), state, part_low, part_high
     )
 
     image = image_near + swap_brick(image_far, 6)
@@ -536,31 +545,31 @@
 
     packed = jnp.zeros((1, 32, TILE), F32)
     grids = []
-    for colour in range(4):
-        given, saved = (near, saved_near) if colour < 2 else (far, saved_far)
+    for colour in range(COLOURS):
+        saved = saved_low if FIRSTS[colour] < SPLIT else saved_high
         grid, packed = run_backward(
-            2 * colour, info, index, given, front, behind, saved, turned, packed
+            colour, info, index, near, far, front, behind, saved, turned, packed
         )
-        grids.append(grid.reshape((2, 2, 4) + grid.shape[2:]))
+        grids.append(grid)
     for flip in (1, 2, 6):
         packed = packed + swap_brick(packed, flip)
     packed = jnp.concatenate([packed[0, :, k * LANES : (k + 1) * LANES] for k in range(4)], axis=0)
     packed = packed[:104]
 
     sources = []
-    for colour in range(4):
+    for colour in range(COLOURS):
         part = grids[colour]
         for turn in range(2):
             part = part[0] + view_swap(part[1], colour, turn)
         part = part.reshape(-1, LANES)
         rows = part.shape[0]
-        if colour == 3:
+        if colour == LAST:
             part = jnp.concatenate([part, packed], axis=0)
         for turn in (2, 3):
             part = part + view_swap(part, colour, turn)
         got = view_swap(part, colour, 1)
         sent = jnp.concatenate([part[:rows], got[:rows]], axis=0)
-        if colour == 3:
+        if colour == LAST:
             packed = part[rows:] + got[rows:]
             sent = jnp.concatenate([sent, packed], axis=0)
         sources += [part, got, view_swap(sent, colour, 0)]

time: 119 us -> 119 us (level)
  waiting for transfers between devices: 36.2 us -> 45.2 us
  starting transfers between devices: 42 us -> 35 us
    ppermute x24 -> x18, waiting for transfers between devices: 15.8 us -> 27.7 us  [view_swap(): return lax.ppermute(array, ('brick', 'view'), pairs)]
    ppermute x24 -> x18, starting transfers between devices: 31.7 us -> 24.9 us  [view_swap(): return lax.ppermute(array, ('brick', 'view'), pairs)]
    ppermute x12 -> x13, waiting for transfers between devices: 20.4 us -> 17.6 us  [swap_brick(): return lax.ppermute(array, 'brick', [(i, i ^ flip) for i in range(8)])]
    ppermute x12 -> x13, starting transfers between devices: 10.3 us -> 10.1 us  [swap_brick(): return lax.ppermute(array, 'brick', [(i, i ^ flip) for i in range(8)])]
    pallas_call x4 -> x3, Pallas kernels: 15.8 us -> 15.6 us  [run_backward(): pl.pallas_call(functools.partial(backward_kernel, colour), out_shape=[jax...]
  transfers between devices with their start and end apart: 36 -> 31, of which waited for: 16 -> 18; matrix products, arithmetic and copies ran while one was open for 2% -> 2% of each run, Pallas kernels for 26% -> 26%
where the time goes in v1:
time: 119 us
  waiting for transfers between devices  45.2 us (38%)
  starting transfers between devices  35 us (29%)
  Pallas kernels  34.9 us (29%)
  between operations  1.64 us (1%)
    ppermute x18, waiting for transfers between devices, view_swap(): return lax.ppermute(array, ('brick', 'view'), pairs)  27.7 us
    ppermute x18, starting transfers between devices, view_swap(): return lax.ppermute(array, ('brick', 'view'), pairs)  24.9 us
    ppermute x13, waiting for transfers between devices, swap_brick(): return lax.ppermute(array, 'brick', [(i, i ^ flip) for i in range(8)])  17.6 us
    pallas_call x3, Pallas kernels, run_backward(): pl.pallas_call(functools.partial(backward_kernel, colour), out_shape=[jax...  15.6 us
    pallas_call x2, Pallas kernels, run_forward(): pl.pallas_call(functools.partial(forward_kernel, first), out_shape=shapes...  13.9 us
    ppermute x13, starting transfers between devices, swap_brick(): return lax.ppermute(array, 'brick', [(i, i ^ flip) for i in range(8)])  10.1 us
  transfers between devices with their start and end apart: 31, of which 18 were waited for; matrix products, arithmetic and copies ran while one was open for 2% of the time, Pallas kernels for 26%

profile of v1, /device:TPU:0, one launch (start us, length us, event | category | flops | bytes accessed | tf_op | source)
XLA Modules:
  0.0 119.2 jit_solution(9186370518255012676)
XLA Ops:
  0.6 2.1 %collective-permute-start.1 = (f32[1,32,512]{2,1,0:T(8,128)}, f32[1,32,512]{2,1,0:T(8,128)S(1)}, u32[]{:S(2)}, u32[]{:S(2)}) collective-permute-start(f32[1,32,512]{2,1,0:T(8,128)} %param.15), channel_id=1, source_target_pairs={{0,32},{16,48},{32,0},{48,16},{64,96},{80,112},{96,64},{112,80},{1... | collective-permute-start | bytes 196616 | tf_op jit(solution)/shard_map/ppermute | solution.py:474
  6.7 3.3 %collective-permute-start.3 = (f32[4,32,512]{2,1,0:T(8,128)S(1)}, f32[4,32,512]{2,1,0:T(8,128)S(1)}, u32[]{:S(2)}, u32[]{:S(2)}) collective-permute-start(f32[4,32,512]{2,1,0:T(8,128)S(1)} %constant_dynamic-update-slice_fusion.near_ref), channel_id=1, source_target_pairs={{0,96},{16,112},{32,64},{48,80},{64,32},{80,48},{96,0},{112,16},{1... | collective-permute-start | bytes 786440 | tf_op jit(solution)/shard_map/ppermute | solution.py:474
  11.6 3.8 %forward.3 = (f32[2,32,512]{2,1,0:T(8,128)S(1)}, f32[2,512]{1,0:T(2,128)S(1)}, bf16[2,6,64,4096]{3,2,1,0:T(8,128)(2,1)S(1)}, bf16[2,16,4096]{2,1,0:T(8,128)(2,1)...) custom-call(s32[8]{0:T(128)S(1)} %stack.26.brick_ref.info_ref, ...), custom_call_target="tpu_custom_call" | custom-call | flops 500000000 | bytes 8000000 | tf_op jit(solution)/shard_map/forward/pallas_call | solution.py:363
  15.3 10.1 %forward.2 = (f32[6,32,512]{2,1,0:T(8,128)S(1)}, f32[6,512]{1,0:T(8,128)S(1)}, bf16[6,6,64,4096]{3,2,1,0:T(8,128)(2,1)S(1)}, bf16[6,16,4096]{2,1,0:T(8,128)(2,1)...) custom-call(s32[8]{0:T(128)S(1)} %stack.26.brick_ref.info_ref, ...), custom_call_target="tpu_custom_call" | custom-call | flops 1500000000 | bytes 24000000 | tf_op jit(solution)/shard_map/forward/pallas_call | solution.py:363
  27.7 3.7 %collective-permute-done.5.got_ref = f32[2,8,512]{2,1,0:T(8,128)S(1)} collective-permute-done((f32[2,8,512]{2,1,0:T(8,128)S(1)}, f32[2,8,512]{2,1,0:T(8,128)S(1)}, u32[]{:S(2)}, u32[]{:S(2)}) %collective-permute-start.5) | collective-permute-done | bytes 32800 | tf_op jit(solution)/shard_map/ppermute | solution.py:474
  32.2 5.0 %collective-permute-done.6.got_ref = f32[2,8,512]{2,1,0:T(8,128)S(1)} collective-permute-done((f32[2,8,512]{2,1,0:T(8,128)S(1)}, f32[2,8,512]{2,1,0:T(8,128)S(1)}, u32[]{:S(2)}, u32[]{:S(2)}) %collective-permute-start.6) | collective-permute-done | bytes 32800 | tf_op jit(solution)/shard_map/ppermute | solution.py:474
  38.0 5.8 %backward.3 = (f32[2,2,3,2,64,128]{5,4,3,2,1,0:T(8,128)S(1)}, f32[1,32,512]{2,1,0:T(8,128)S(1)}) custom-call(s32[8]{0:T(128)S(1)} %stack.26.brick_ref.info_ref, s32[8,4096]{1,0:T(8,128)S(1)} %get-tuple-element.48.samples_ref, f32[4,32,512]{2,1,0:T(8,128)S(1)} %constant_dynamic-update-slice_fusion.near_ref, f32[4,32,512]{2,1,0:T(8,128)S(1)} %collective-permute-done.3.far_ref, ...), custom_call_target="tpu_custom_call" | custom-call | flops 1500000000 | bytes 13500000 | tf_op jit(solution)/shard_map/backward/pallas_call | solution.py:410
  43.7 5.8 %backward.4 = (f32[2,2,3,2,64,128]{5,4,3,2,1,0:T(8,128)S(1)}, f32[1,32,512]{2,1,0:T(8,128)S(1)}) custom-call(s32[8]{0:T(128)S(1)} %stack.26.brick_ref.info_ref, s32[8,4096]{1,0:T(8,128)S(1)} %get-tuple-element.48.samples_ref, f32[4,32,512]{2,1,0:T(8,128)S(1)} %constant_dynamic-update-slice_fusion.near_ref, f32[4,32,512]{2,1,0:T(8,128)S(1)} %collective-permute-done.3.far_ref, ...), custom_call_target="tpu_custom_call" | custom-call | flops 1500000000 | bytes 13500000 | tf_op jit(solution)/shard_map/backward/pallas_call | solution.py:410
  49.5 4.1 %backward.5 = (f32[2,2,2,2,64,128]{5,4,3,2,1,0:T(8,128)S(1)}, f32[1,32,512]{2,1,0:T(8,128)S(1)}) custom-call(s32[8]{0:T(128)S(1)} %stack.26.brick_ref.info_ref, s32[8,4096]{1,0:T(8,128)S(1)} %get-tuple-element.48.samples_ref, f32[4,32,512]{2,1,0:T(8,128)S(1)} %constant_dynamic-update-slice_fusion.near_ref, f32[4,32,512]{2,1,0:T(8,128)S(1)} %collective-permute-done.3.far_ref, ...), custom_call_target="tpu_custom_call" | custom-call | flops 1000000000 | bytes 9000000 | tf_op jit(solution)/shard_map/backward/pallas_call | solution.py:410
  55.4 4.4 %collective-permute-done.25 = f32[1,32,512]{2,1,0:T(8,128)S(1)} collective-permute-done((f32[1,32,512]{2,1,0:T(8,128)S(1)}, f32[1,32,512]{2,1,0:T(8,128)S(1)}, u32[]{:S(2)}, u32[]{:S(2)}) %collective-permute-start.25) | collective-permute-done | bytes 65568 | tf_op jit(solution)/shard_map/ppermute | solution.py:474
  59.8 3.2 %collective-permute-start.26 = (f32[1,32,512]{2,1,0:T(8,128)S(1)}, f32[1,32,512]{2,1,0:T(8,128)S(1)}, u32[]{:S(2)}, u32[]{:S(2)}) collective-permute-start(f32[1,32,512]{2,1,0:T(8,128)S(1)} %add.71), channel_id=1, source_target_pairs={{0,96},{16,112},{32,64},{48,80},{64,32},{80,48},{96,0},{112,16},{1... | collective-permute-start | bytes 196616 | tf_op jit(solution)/shard_map/ppermute | solution.py:474
  64.4 1.9 %collective-permute-start.16 = (f32[2,3,2,64,128]{4,3,2,1,0:T(8,128)S(1)}, f32[2,3,2,64,128]{4,3,2,1,0:T(8,128)S(1)}, u32[]{:S(2)}, u32[]{:S(2)}) collective-permute-start(f32[2,3,2,64,128]{4,3,2,1,0:T(8,128)S(1)} %slice_bitcast_fusion), channel_id=1, source_target_pairs={{0,3},{16,17},{32,35},{48,49},{64,67},{80,81},{96,99},{112,113},{1... | collective-permute-start | bytes 1179656 | tf_op jit(solution)/shard_map/ppermute | solution.py:490
  66.4 1.8 %collective-permute-start.23 = (f32[2,2,64,128]{3,2,1,0:T(8,128)S(1)}, f32[2,2,64,128]{3,2,1,0:T(8,128)S(1)}, u32[]{:S(2)}, u32[]{:S(2)}) collective-permute-start(f32[2,2,64,128]{3,2,1,0:T(8,128)S(1)} %slice_bitcast_fusion.7), channel_id=1, source_target_pairs={{0,4},{16,28},{32,36},{48,60},{64,68},{80,92},{96,100},{112,124},{... | collective-permute-start | bytes 393224 | tf_op jit(solution)/shard_map/ppermute | solution.py:490
  68.4 3.2 %collective-permute-done.23 = f32[2,2,64,128]{3,2,1,0:T(8,128)S(1)} collective-permute-done((f32[2,2,64,128]{3,2,1,0:T(8,128)S(1)}, f32[2,2,64,128]{3,2,1,0:T(8,128)S(1)}, u32[]{:S(2)}, u32[]{:S(2)}) %collective-permute-start.23) | collective-permute-done | bytes 131104 | tf_op jit(solution)/shard_map/ppermute | solution.py:490
  73.1 2.1 %collective-permute-done.10 = f32[2,3,2,64,128]{4,3,2,1,0:T(8,128)S(1)} collective-permute-done((f32[2,3,2,64,128]{4,3,2,1,0:T(8,128)S(1)}, f32[2,3,2,64,128]{4,3,2,1,0:T(8,128)S(1)}, u32[]{:S(2)}, u32[]{:S(2)}) %collective-permute-start.10) | collective-permute-done | bytes 393248 | tf_op jit(solution)/shard_map/ppermute | solution.py:490
  77.0 2.2 %collective-permute-start.17 = (f32[3,2,64,128]{3,2,1,0:T(8,128)S(1)}, f32[3,2,64,128]{3,2,1,0:T(8,128)S(1)}, u32[]{:S(2)}, u32[]{:S(2)}) collective-permute-start(f32[3,2,64,128]{3,2,1,0:T(8,128)S(1)} %slice_bitcast_fusion.3), channel_id=1, source_target_pairs={{0,12},{16,20},{32,44},{48,52},{64,76},{80,84},{96,108},{112,116},... | collective-permute-start | bytes 589832 | tf_op jit(solution)/shard_map/ppermute | solution.py:490
  79.3 2.3 %collective-permute-start.28 = (f32[360,128]{1,0:T(8,128)S(1)}, f32[360,128]{1,0:T(8,128)S(1)}, u32[]{:S(2)}, u32[]{:S(2)}) collective-permute-start(f32[360,128]{1,0:T(8,128)S(1)} %add.73), channel_id=1, source_target_pairs={{0,12},{16,20},{32,44},{48,52},{64,76},{80,84},{96,108},{112,116},... | collective-permute-start | bytes 552968 | tf_op jit(solution)/shard_map/ppermute | solution.py:490
  82.8 2.6 %collective-permute-start.12 = (f32[384,128]{1,0:T(8,128)S(1)}, f32[384,128]{1,0:T(8,128)S(1)}, u32[]{:S(2)}, u32[]{:S(2)}) collective-permute-start(f32[384,128]{1,0:T(8,128)S(1)} %bitcast.53), channel_id=1, source_target_pairs={{0,3},{16,17},{32,35},{48,49},{64,67},{80,81},{96,99},{112,113},{1... | collective-permute-start | bytes 589832 | tf_op jit(solution)/shard_map/ppermute | solution.py:490
  87.2 4.1 %collective-permute-done.12 = f32[384,128]{1,0:T(8,128)S(1)} collective-permute-done((f32[384,128]{1,0:T(8,128)S(1)}, f32[384,128]{1,0:T(8,128)S(1)}, u32[]{:S(2)}, u32[]{:S(2)}) %collective-permute-start.12) | collective-permute-done | bytes 196640 | tf_op jit(solution)/shard_map/ppermute | solution.py:490
  93.5 7.0 %collective-permute-done.13 = f32[384,128]{1,0:T(8,128)S(1)} collective-permute-done((f32[384,128]{1,0:T(8,128)S(1)}, f32[384,128]{1,0:T(8,128)S(1)}, u32[]{:S(2)}, u32[]{:S(2)}) %collective-permute-start.13) | collective-permute-done | bytes 196640 | tf_op jit(solution)/shard_map/ppermute | solution.py:490
  102.5 3.7 %collective-permute-done.14.refs_1_ = f32[384,128]{1,0:T(8,128)S(1)} collective-permute-done((f32[384,128]{1,0:T(8,128)S(1)}, f32[384,128]{1,0:T(8,128)S(1)}, u32[]{:S(2)}, u32[]{:S(2)}) %collective-permute-start.14) | collective-permute-done | bytes 196640 | tf_op jit(solution)/shard_map/ppermute | solution.py:490
  107.6 2.7 %collective-permute-start.21 = (f32[768,128]{1,0:T(8,128)S(1)}, f32[768,128]{1,0:T(8,128)S(1)}, u32[]{:S(2)}, u32[]{:S(2)}) collective-permute-start(f32[768,128]{1,0:T(8,128)S(1)} %pad_maximum_fusion.1), channel_id=1, source_target_pairs={{0,3},{16,17},{32,35},{48,49},{64,67},{80,81},{96,99},{112,113},{1... | collective-permute-start | bytes 1179656 | tf_op jit(solution)/shard_map/ppermute | solution.py:490
  112.8 4.2 %collective-permute-done.15.refs_2_ = f32[768,128]{1,0:T(8,128)S(1)} collective-permute-done((f32[768,128]{1,0:T(8,128)S(1)}, f32[768,128]{1,0:T(8,128)S(1)}, u32[]{:S(2)}, u32[]{:S(2)}) %collective-permute-start.15) | collective-permute-done | bytes 393248 | tf_op jit(solution)/shard_map/ppermute | solution.py:490
  117.0 2.2 %finish.1 = (f32[1,16,32768]{2,1,0:T(8,128)}, f32[16,64]{1,0:T(8,128)}, f32[64,64]{1,0:T(8,128)}, f32[64,64]{1,0:T(8,128)}, f32[33,64]{1,0:T(8,128)}) custom-call(s32[8]{0:T(128)S(1)} %stack.26.brick_ref.info_ref, f32[384,128]{1,0:T(8,128)S(1)} %add.63.refs_0_, f32[384,128]{1,0:T(8,128)S(1)} %collective-permute-done.14.refs_1_, ...), custom_call_target="tpu_custom_call" | custom-call | tf_op jit(solution)/shard_map/finish/pallas_call | solution.py:457
  (89 shorter events, 26.2 us)
Async XLA Ops:
  0.6 4.7 %collective-permute-start.1 = (f32[1,32,512]{2,1,0:T(8,128)}, f32[1,32,512]{2,1,0:T(8,128)S(1)}, u32[]{:S(2)}, u32[]{:S(2)}) collective-permute-start(f32[1,32,512]{2,1,0:T(8,128)} %param.15), channel_id=1, source_target_pairs={{0,32},{16,48},{32,0},{48,16},{64,96},{80,112},{96,64},{112,80},{1... | collective-permute-start | bytes 196616 | tf_op jit(solution)/shard_map/ppermute | solution.py:474
  6.7 18.8 %collective-permute-start.3 = (f32[4,32,512]{2,1,0:T(8,128)S(1)}, f32[4,32,512]{2,1,0:T(8,128)S(1)}, u32[]{:S(2)}, u32[]{:S(2)}) collective-permute-start(f32[4,32,512]{2,1,0:T(8,128)S(1)} %constant_dynamic-update-slice_fusion.near_ref), channel_id=1, source_target_pairs={{0,96},{16,112},{32,64},{48,80},{64,32},{80,48},{96,0},{112,16},{1... | collective-permute-start | bytes 786440 | tf_op jit(solution)/shard_map/ppermute | solution.py:474
  32.0 5.2 %collective-permute-start.6 = (f32[2,8,512]{2,1,0:T(8,128)S(1)}, f32[2,8,512]{2,1,0:T(8,128)S(1)}, u32[]{:S(2)}, u32[]{:S(2)}) collective-permute-start(f32[2,8,512]{2,1,0:T(8,128)S(1)} %get-tuple-element.59.own_ref), channel_id=1, source_target_pairs={{0,96},{16,112},{32,64},{48,80},{64,32},{80,48},{96,0},{112,16},{1... | collective-permute-start | bytes 98312 | tf_op jit(solution)/shard_map/ppermute | solution.py:474
  37.8 30.4 %collective-permute-start.7 = (f32[4,32,512]{2,1,0:T(8,128)S(1)}, f32[4,32,512]{2,1,0:T(8,128)S(1)}, u32[]{:S(2)}, u32[]{:S(2)}) collective-permute-start(f32[4,32,512]{2,1,0:T(8,128)S(1)} %get-tuple-element.62), channel_id=1, source_target_pairs={{0,96},{16,112},{32,64},{48,80},{64,32},{80,48},{96,0},{112,16},{1... | collective-permute-start | bytes 786440 | tf_op jit(solution)/shard_map/ppermute | solution.py:474
  53.7 12.6 %collective-permute-start.22 = (f32[2,2,2,64,128]{4,3,2,1,0:T(8,128)S(1)}, f32[2,2,2,64,128]{4,3,2,1,0:T(8,128)S(1)}, u32[]{:S(2)}, u32[]{:S(2)}) collective-permute-start(f32[2,2,2,64,128]{4,3,2,1,0:T(8,128)S(1)} %slice_bitcast_fusion.2), channel_id=1, source_target_pairs={{0,1},{16,19},{32,33},{48,51},{64,65},{80,83},{96,97},{112,115},{1... | collective-permute-start | bytes 786440 | tf_op jit(solution)/shard_map/ppermute | solution.py:490
  59.8 6.4 %collective-permute-start.26 = (f32[1,32,512]{2,1,0:T(8,128)S(1)}, f32[1,32,512]{2,1,0:T(8,128)S(1)}, u32[]{:S(2)}, u32[]{:S(2)}) collective-permute-start(f32[1,32,512]{2,1,0:T(8,128)S(1)} %add.71), channel_id=1, source_target_pairs={{0,96},{16,112},{32,64},{48,80},{64,32},{80,48},{96,0},{112,16},{1... | collective-permute-start | bytes 196616 | tf_op jit(solution)/shard_map/ppermute | solution.py:474
  63.1 12.1 %collective-permute-start.10 = (f32[2,3,2,64,128]{4,3,2,1,0:T(8,128)S(1)}, f32[2,3,2,64,128]{4,3,2,1,0:T(8,128)S(1)}, u32[]{:S(2)}, u32[]{:S(2)}) collective-permute-start(f32[2,3,2,64,128]{4,3,2,1,0:T(8,128)S(1)} %slice_bitcast_fusion.1), channel_id=1, source_target_pairs={{0,1},{16,19},{32,33},{48,51},{64,65},{80,83},{96,97},{112,115},{1... | collective-permute-start | bytes 1179656 | tf_op jit(solution)/shard_map/ppermute | solution.py:490
  64.4 12.5 %collective-permute-start.16 = (f32[2,3,2,64,128]{4,3,2,1,0:T(8,128)S(1)}, f32[2,3,2,64,128]{4,3,2,1,0:T(8,128)S(1)}, u32[]{:S(2)}, u32[]{:S(2)}) collective-permute-start(f32[2,3,2,64,128]{4,3,2,1,0:T(8,128)S(1)} %slice_bitcast_fusion), channel_id=1, source_target_pairs={{0,3},{16,17},{32,35},{48,49},{64,67},{80,81},{96,99},{112,113},{1... | collective-permute-start | bytes 1179656 | tf_op jit(solution)/shard_map/ppermute | solution.py:490
  66.4 5.2 %collective-permute-start.23 = (f32[2,2,64,128]{3,2,1,0:T(8,128)S(1)}, f32[2,2,64,128]{3,2,1,0:T(8,128)S(1)}, u32[]{:S(2)}, u32[]{:S(2)}) collective-permute-start(f32[2,2,64,128]{3,2,1,0:T(8,128)S(1)} %slice_bitcast_fusion.7), channel_id=1, source_target_pairs={{0,4},{16,28},{32,36},{48,60},{64,68},{80,92},{96,100},{112,124},{... | collective-permute-start | bytes 393224 | tf_op jit(solution)/shard_map/ppermute | solution.py:490
  68.3 42.1 %collective-permute-start.8 = (f32[2,32,512]{2,1,0:T(8,128)S(1)}, f32[2,32,512]{2,1,0:T(8,128)S(1)}, u32[]{:S(2)}, u32[]{:S(2)}) collective-permute-start(f32[2,32,512]{2,1,0:T(8,128)S(1)} %slice.101), channel_id=1, source_target_pairs={{0,32},{16,48},{32,0},{48,16},{64,96},{80,112},{96,64},{112,80},{1... | collective-permute-start | bytes 393224 | tf_op jit(solution)/shard_map/ppermute | solution.py:474
  71.6 7.6 %collective-permute-start.27 = (f32[360,128]{1,0:T(8,128)S(1)}, f32[360,128]{1,0:T(8,128)S(1)}, u32[]{:S(2)}, u32[]{:S(2)}) collective-permute-start(f32[360,128]{1,0:T(8,128)S(1)} %fusion.2), channel_id=1, source_target_pairs={{0,3},{16,17},{32,35},{48,49},{64,67},{80,81},{96,99},{112,113},{1... | collective-permute-start | bytes 552968 | tf_op jit(solution)/shard_map/ppermute | solution.py:490
  75.2 7.5 %collective-permute-start.11 = (f32[3,2,64,128]{3,2,1,0:T(8,128)S(1)}, f32[3,2,64,128]{3,2,1,0:T(8,128)S(1)}, u32[]{:S(2)}, u32[]{:S(2)}) collective-permute-start(f32[3,2,64,128]{3,2,1,0:T(8,128)S(1)} %slice_bitcast_fusion.5), channel_id=1, source_target_pairs={{0,4},{16,28},{32,36},{48,60},{64,68},{80,92},{96,100},{112,124},{... | collective-permute-start | bytes 589832 | tf_op jit(solution)/shard_map/ppermute | solution.py:490
  77.0 8.4 %collective-permute-start.17 = (f32[3,2,64,128]{3,2,1,0:T(8,128)S(1)}, f32[3,2,64,128]{3,2,1,0:T(8,128)S(1)}, u32[]{:S(2)}, u32[]{:S(2)}) collective-permute-start(f32[3,2,64,128]{3,2,1,0:T(8,128)S(1)} %slice_bitcast_fusion.3), channel_id=1, source_target_pairs={{0,12},{16,20},{32,44},{48,52},{64,76},{80,84},{96,108},{112,116},... | collective-permute-start | bytes 589832 | tf_op jit(solution)/shard_map/ppermute | solution.py:490
  79.3 6.8 %collective-permute-start.28 = (f32[360,128]{1,0:T(8,128)S(1)}, f32[360,128]{1,0:T(8,128)S(1)}, u32[]{:S(2)}, u32[]{:S(2)}) collective-permute-start(f32[360,128]{1,0:T(8,128)S(1)} %add.73), channel_id=1, source_target_pairs={{0,12},{16,20},{32,44},{48,52},{64,76},{80,84},{96,108},{112,116},... | collective-permute-start | bytes 552968 | tf_op jit(solution)/shard_map/ppermute | solution.py:490
  82.8 8.6 %collective-permute-start.12 = (f32[384,128]{1,0:T(8,128)S(1)}, f32[384,128]{1,0:T(8,128)S(1)}, u32[]{:S(2)}, u32[]{:S(2)}) collective-permute-start(f32[384,128]{1,0:T(8,128)S(1)} %bitcast.53), channel_id=1, source_target_pairs={{0,3},{16,17},{32,35},{48,49},{64,67},{80,81},{96,99},{112,113},{1... | collective-permute-start | bytes 589832 | tf_op jit(solution)/shard_map/ppermute | solution.py:490
  85.4 7.8 %collective-permute-start.18 = (f32[384,128]{1,0:T(8,128)S(1)}, f32[384,128]{1,0:T(8,128)S(1)}, u32[]{:S(2)}, u32[]{:S(2)}) collective-permute-start(f32[384,128]{1,0:T(8,128)S(1)} %bitcast.54), channel_id=1, source_target_pairs={{0,1},{16,19},{32,33},{48,51},{64,65},{80,83},{96,97},{112,115},{1... | collective-permute-start | bytes 589832 | tf_op jit(solution)/shard_map/ppermute | solution.py:490
  86.1 14.4 %collective-permute-start.29 = (f32[360,128]{1,0:T(8,128)S(1)}, f32[360,128]{1,0:T(8,128)S(1)}, u32[]{:S(2)}, u32[]{:S(2)}) collective-permute-start(f32[360,128]{1,0:T(8,128)S(1)} %add.74.refs_6_), channel_id=1, source_target_pairs={{0,4},{16,28},{32,36},{48,60},{64,68},{80,92},{96,100},{112,124},{... | collective-permute-start | bytes 552968 | tf_op jit(solution)/shard_map/ppermute | solution.py:490
  91.4 9.1 %collective-permute-start.13 = (f32[384,128]{1,0:T(8,128)S(1)}, f32[384,128]{1,0:T(8,128)S(1)}, u32[]{:S(2)}, u32[]{:S(2)}) collective-permute-start(f32[384,128]{1,0:T(8,128)S(1)} %bitcast_add_fusion.4), channel_id=1, source_target_pairs={{0,12},{16,20},{32,44},{48,52},{64,76},{80,84},{96,108},{112,116},... | collective-permute-start | bytes 589832 | tf_op jit(solution)/shard_map/ppermute | solution.py:490
  93.2 7.4 %collective-permute-start.19 = (f32[384,128]{1,0:T(8,128)S(1)}, f32[384,128]{1,0:T(8,128)S(1)}, u32[]{:S(2)}, u32[]{:S(2)}) collective-permute-start(f32[384,128]{1,0:T(8,128)S(1)} %bitcast_add_fusion.3), channel_id=1, source_target_pairs={{0,4},{16,28},{32,36},{48,60},{64,68},{80,92},{96,100},{112,124},{... | collective-permute-start | bytes 589832 | tf_op jit(solution)/shard_map/ppermute | solution.py:490
  100.4 5.7 %collective-permute-start.14 = (f32[384,128]{1,0:T(8,128)S(1)}, f32[384,128]{1,0:T(8,128)S(1)}, u32[]{:S(2)}, u32[]{:S(2)}) collective-permute-start(f32[384,128]{1,0:T(8,128)S(1)} %add.63.refs_0_), channel_id=1, source_target_pairs={{0,4},{16,28},{32,36},{48,60},{64,68},{80,92},{96,100},{112,124},{... | collective-permute-start | bytes 589832 | tf_op jit(solution)/shard_map/ppermute | solution.py:490
  100.6 7.0 %collective-permute-start.20 = (f32[384,128]{1,0:T(8,128)S(1)}, f32[384,128]{1,0:T(8,128)S(1)}, u32[]{:S(2)}, u32[]{:S(2)}) collective-permute-start(f32[384,128]{1,0:T(8,128)S(1)} %add.67.refs_3_), channel_id=1, source_target_pairs={{0,12},{16,20},{32,44},{48,52},{64,76},{80,84},{96,108},{112,116},... | collective-permute-start | bytes 589832 | tf_op jit(solution)/shard_map/ppermute | solution.py:490
  102.4 10.3 %collective-permute-start.30 = (f32[616,128]{1,0:T(8,128)S(1)}, f32[616,128]{1,0:T(8,128)S(1)}, u32[]{:S(2)}, u32[]{:S(2)}) collective-permute-start(f32[616,128]{1,0:T(8,128)S(1)} %pad_maximum_fusion.2), channel_id=1, source_target_pairs={{0,1},{16,19},{32,33},{48,51},{64,65},{80,83},{96,97},{112,115},{1... | collective-permute-start | bytes 946184 | tf_op jit(solution)/shard_map/ppermute | solution.py:490
  106.2 10.8 %collective-permute-start.15 = (f32[768,128]{1,0:T(8,128)S(1)}, f32[768,128]{1,0:T(8,128)S(1)}, u32[]{:S(2)}, u32[]{:S(2)}) collective-permute-start(f32[768,128]{1,0:T(8,128)S(1)} %pad_maximum_fusion), channel_id=1, source_target_pairs={{0,1},{16,19},{32,33},{48,51},{64,65},{80,83},{96,97},{112,115},{1... | collective-permute-start | bytes 1179656 | tf_op jit(solution)/shard_map/ppermute | solution.py:490
  107.6 9.4 %collective-permute-start.21 = (f32[768,128]{1,0:T(8,128)S(1)}, f32[768,128]{1,0:T(8,128)S(1)}, u32[]{:S(2)}, u32[]{:S(2)}) collective-permute-start(f32[768,128]{1,0:T(8,128)S(1)} %pad_maximum_fusion.1), channel_id=1, source_target_pairs={{0,3},{16,17},{32,35},{48,49},{64,67},{80,81},{96,99},{112,113},{1... | collective-permute-start | bytes 1179656 | tf_op jit(solution)/shard_map/ppermute | solution.py:490
  (7 other events, 18.2 us)

commit v2 on v1

--- a/solution.py
+++ b/solution.py
@@ -20,7 +20,7 @@
 FIRSTS = tuple(sum(SIZES[:c]) for c in range(len(SIZES)))
 COLOURS = len(SIZES)
 LAST = COLOURS - 1
-SPLIT = 6
+SPLIT = 3
 
 
 def mm(a, b):
@@ -194,12 +194,13 @@
 
 
 def prepare_kernel(
-    grid_in_ref, samples_in_ref, one_t_in_ref, two_in_ref, three_in_ref, four_in_ref,
-    grid_ref, samples_ref, one_ref, two_ref, three_ref, four_ref,
+    grid_in_ref, samples_in_ref, given_in_ref, one_t_in_ref, two_in_ref, three_in_ref, four_in_ref,
+    grid_ref, samples_ref, given_ref, one_ref, two_ref, three_ref, four_ref,
     one_t_ref, two_t_ref, three_t_ref, four_t_ref,
 ):
     grid_ref[...] = grid_in_ref[...]
     samples_ref[...] = samples_in_ref[...]
+    given_ref[...] = given_in_ref[...]
     one_t = one_t_in_ref[...].astype(F32) * 0.5
     one_ref[...] = one_t.T.astype(BF16)
     one_t_ref[...] = one_t.astype(BF16)
@@ -233,35 +234,51 @@
         out_ref[1, p : p + 1, :] = jnp.sum(given * part, axis=0, keepdims=True)
 
 
-def merge_kernel(level, flip, info_ref, order_ref, own_ref, got_ref, *refs):
+def first_of(rank, level, shape):
+    bit = jnp.bitwise_and(jnp.right_shift(rank, level), 1)
+    return jnp.full(shape, bit, jnp.int32) == 0
+
+
+def joined(first, total, dots, other_total, other_dots):
+    return total * other_total, jnp.where(
+        first, dots + total * other_dots, other_dots + other_total * dots
+    )
+
+
+def quad_kernel(info_ref, order_ref, own_ref, one_ref, two_ref, three_ref, out_ref, next_ref):
     total, dots = own_ref[0], own_ref[1]
-    got_total = flip_rows(got_ref[0], flip)
-    got_dots = flip_rows(got_ref[1], flip)
     rank = jnp.bitwise_xor(info_ref[0], order_ref[0])
-    bit = jnp.bitwise_and(jnp.right_shift(rank, level), 1)
-    first = jnp.full(total.shape, bit, jnp.int32) == 0
-    if level == 0:
-        front, after, behind = jnp.ones_like(total), jnp.ones_like(total), jnp.zeros_like(total)
-    else:
-        state_ref, *refs = refs
-        front, after, behind = state_ref[0], state_ref[1], state_ref[2]
-    behind = jnp.where(first, behind + after * got_dots, behind)
-    front = jnp.where(first, front, front * got_total)
-    if level < 2:
-        out_ref, next_ref = refs
-        next_ref[0] = front
-        next_ref[1] = jnp.where(first, after * got_total, after)
-        next_ref[2] = behind
-        out_ref[0] = total * got_total
-        out_ref[1] = jnp.where(first, dots + total * got_dots, got_dots + got_total * dots)
-    else:
-        part_low_ref, part_high_ref, front_ref, behind_ref, image_near_ref, image_far_ref = refs
-        front_ref[...] = front
-        behind_ref[...] = behind
-        for p in range(8):
-            part = part_low_ref[p] if p < SPLIT else part_high_ref[p - SPLIT]
-            image_ref = image_near_ref if p < 4 else image_far_ref
-            image_ref[p % 4] = front[p : p + 1] * part
+    ones, zeros = jnp.ones_like(total), jnp.zeros_like(total)
+    first = first_of(rank, 0, total.shape)
+    one_total, one_dots = (flip_rows(one_ref[i], 1) for i in range(2))
+    two_total, two_dots = (flip_rows(two_ref[i], 2) for i in range(2))
+    three_total, three_dots = (flip_rows(flip_rows(three_ref[i], 1), 2) for i in range(2))
+    behind = jnp.where(first, one_dots, zeros)
+    after = jnp.where(first, one_total, ones)
+    front = jnp.where(first, ones, one_total)
+    total, dots = joined(first, total, dots, one_total, one_dots)
+    other_total, other_dots = joined(first, two_total, two_dots, three_total, three_dots)
+    first = first_of(rank, 1, total.shape)
+    next_ref[0] = jnp.where(first, front, front * other_total)
+    next_ref[1] = jnp.where(first, behind + after * other_dots, behind)
+    next_ref[2] = jnp.where(first, after * other_total, after)
+    out_ref[0], out_ref[1] = joined(first, total, dots, other_total, other_dots)
+
+
+def eight_kernel(
+    info_ref, order_ref, got_ref, state_ref, part_low_ref, part_high_ref,
+    front_ref, behind_ref, image_near_ref, image_far_ref,
+):
+    got_total, got_dots = flip_rows(got_ref[0], 4), flip_rows(got_ref[1], 4)
+    rank = jnp.bitwise_xor(info_ref[0], order_ref[0])
+    first = first_of(rank, 2, got_total.shape)
+    front = jnp.where(first, state_ref[0], state_ref[0] * got_total)
+    front_ref[...] = front
+    behind_ref[...] = jnp.where(first, state_ref[1] + state_ref[2] * got_dots, state_ref[1])
+    for p in range(8):
+        part = part_low_ref[p] if p < SPLIT else part_high_ref[p - SPLIT]
+        image_ref = image_near_ref if p < 4 else image_far_ref
+        image_ref[p % 4] = front[p : p + 1] * part
 
 
 def finish_kernel(info_ref, *refs):
@@ -297,7 +314,7 @@
 SMALL = pltpu.CompilerParams(vmem_limit_bytes=4 * 2**20)
 
 
-def run_prepare(grid, samples, one_t, two, three, four):
+def run_prepare(grid, samples, given, one_t, two, three, four):
     channels = one_t.shape[0]
     shapes = [(64, channels), (64, 64), (64, 64), (OUT_ROWS, 64)]
     shapes += [shape[::-1] for shape in shapes]
@@ -306,13 +323,14 @@
         out_shape=[
             jax.ShapeDtypeStruct(grid.shape, grid.dtype),
             jax.ShapeDtypeStruct(samples.shape, samples.dtype),
+            jax.ShapeDtypeStruct(given.shape, given.dtype),
             *[jax.ShapeDtypeStruct(shape, BF16) for shape in shapes],
         ],
-        in_specs=[VMEM] * 6,
-        out_specs=[VMEM] * 10,
+        in_specs=[VMEM] * 7,
+        out_specs=[VMEM] * 11,
         compiler_params=SMALL,
         name="prepare",
-    )(grid, samples, one_t, two, three, four)
+    )(grid, samples, given, one_t, two, three, four)
 
 
 def run_dots(*arrays):
@@ -326,19 +344,27 @@
     )(*arrays)
 
 
-def run_merge(level, flip, info, order, own, got, *more):
-    shapes = {
-        False: [(2, 8, TILE), (3, 8, TILE)],
-        True: [(8, TILE), (8, TILE), (4, 32, TILE), (4, 32, TILE)],
-    }[level == 2]
+def run_quad(info, order, *arrays):
     return pl.pallas_call(
-        functools.partial(merge_kernel, level, flip),
+        quad_kernel,
+        out_shape=[jax.ShapeDtypeStruct((n, 8, TILE), F32) for n in (2, 3)],
+        in_specs=[SMEM, SMEM] + [VMEM] * 4,
+        out_specs=[VMEM] * 2,
+        compiler_params=SMALL,
+        name="quad",
+    )(info, order, *arrays)
+
+
+def run_eight(info, order, *arrays):
+    shapes = [(8, TILE), (8, TILE), (4, 32, TILE), (4, 32, TILE)]
+    return pl.pallas_call(
+        eight_kernel,
         out_shape=[jax.ShapeDtypeStruct(shape, F32) for shape in shapes],
-        in_specs=[SMEM, SMEM] + [VMEM] * (2 + len(more)),
-        out_specs=[VMEM] * len(shapes),
+        in_specs=[SMEM, SMEM] + [VMEM] * 4,
+        out_specs=[VMEM] * 4,
         compiler_params=SMALL,
-        name="merge",
-    )(info, order, own, got, *more)
+        name="eight",
+    )(info, order, *arrays)
 
 
 def whole(shape):
@@ -399,7 +425,7 @@
 def run_backward(colour, brick, samples, near, far, weight, behind, saved, layers, before):
     count = SIZES[colour]
     first = FIRSTS[colour]
-    skip = first % SPLIT
+    skip = first if first < SPLIT else first - SPLIT
     wide = STEPS * TILE
     hidden, feature, shade, ray = saved
     channels = feature.shape[1]
@@ -516,27 +542,27 @@
     info = make_info(brick)
     voxels = latent_grid.shape[2]
 
-    latent, index, *layers = run_prepare(
+    latent, index, given, *layers = run_prepare(
         *[
             pltpu.with_memory_space_constraint(array, pltpu.HBM)
             for array in (
-                latent_grid[0], samples[0, 0], layer_one.T, layer_two, layer_three, layer_four,
+                latent_grid[0], samples[0, 0], pixel_grad, layer_one.T, layer_two, layer_three, layer_four,
             )
         ]
     )
     plain, turned = layers[:4], layers[4:]
 
-    near = [pixel_grad] + [swap_brick(pixel_grad, flip) for flip in (1, 2, 3)]
+    near = [given] + [swap_brick(pixel_grad, flip) for flip in (1, 2, 3)]
     part_low, trans_low, *saved_low = run_forward(0, SPLIT, info, latent, index, *plain)
     near = jnp.concatenate(near, axis=0)
     far = swap_brick(near, 6)
     part_high, trans_high, *saved_high = run_forward(SPLIT, 8 - SPLIT, info, latent, index, *plain)
 
     own = run_dots(near, far, part_low, part_high, trans_low, trans_high)
-    own, state = run_merge(0, 1, info, view_order, own, swap_brick(own, 1))
-    own, state = run_merge(1, 2, info, view_order, own, swap_brick(own, 2), state)
-    front, behind, image_near, image_far = run_merge(
-        2, 4, info, view_order, own, swap_brick(own, 6), state, part_low, part_high
+    got = [swap_brick(own, flip) for flip in (2, 3, 1)]
+    own, state = run_quad(info, view_order, own, got[2], got[0], got[1])
+    front, behind, image_near, image_far = run_eight(
+        info, view_order, swap_brick(own, 6), state, part_low, part_high
     )
 
     image = image_near + swap_brick(image_far, 6)
@@ -551,8 +577,9 @@
             colour, info, index, near, far, front, behind, saved, turned, packed
         )
         grids.append(grid)
-    for flip in (1, 2, 6):
-        packed = packed + swap_brick(packed, flip)
+    got = [swap_brick(packed, flip) for flip in (1, 2, 3)]
+    packed = packed + got[0] + (got[1] + got[2])
+    packed = packed + swap_brick(packed, 6)
     packed = jnp.concatenate([packed[0, :, k * LANES : (k + 1) * LANES] for k in range(4)], axis=0)
     packed = packed[:104]
 

time: 119 us -> 116 us (0.975)
  starting transfers between devices: 35 us -> 33.5 us
    ppermute x18, starting transfers between devices: 24.9 us -> 20 us  [view_swap(): return lax.ppermute(array, ('brick', 'view'), pairs)]
    ppermute x13 -> x15, starting transfers between devices: 10.1 us -> 13.5 us  [swap_brick(): return lax.ppermute(array, 'brick', [(i, i ^ flip) for i in range(8)])]
    ppermute x13 -> x15, waiting for transfers between devices: 17.6 us -> 15.7 us  [swap_brick(): return lax.ppermute(array, 'brick', [(i, i ^ flip) for i in range(8)])]
    ppermute x18, waiting for transfers between devices: 27.7 us -> 29 us  [view_swap(): return lax.ppermute(array, ('brick', 'view'), pairs)]
  transfers between devices with their start and end apart: 31 -> 33, of which waited for: 18 -> 16; matrix products, arithmetic and copies ran while one was open for 2% -> 1% of each run, Pallas kernels for 26% -> 13%
where the time goes in v2:
time: 116 us
  waiting for transfers between devices  44.6 us (38%)
  Pallas kernels  34.5 us (30%)
  starting transfers between devices  33.5 us (29%)
  between operations  1.68 us (1%)
  other arithmetic  1.2 us (1%)
    ppermute x18, waiting for transfers between devices, view_swap(): return lax.ppermute(array, ('brick', 'view'), pairs)  29 us
    ppermute x18, starting transfers between devices, view_swap(): return lax.ppermute(array, ('brick', 'view'), pairs)  20 us
    ppermute x15, waiting for transfers between devices, swap_brick(): return lax.ppermute(array, 'brick', [(i, i ^ flip) for i in range(8)])  15.7 us
    pallas_call x3, Pallas kernels, run_backward(): pl.pallas_call(functools.partial(backward_kernel, colour), out_shape=[jax...  15.6 us
    pallas_call x2, Pallas kernels, run_forward(): pl.pallas_call(functools.partial(forward_kernel, first), out_shape=shapes...  13.9 us
    ppermute x15, starting transfers between devices, swap_brick(): return lax.ppermute(array, 'brick', [(i, i ^ flip) for i in range(8)])  13.5 us
  transfers between devices with their start and end apart: 33, of which 16 were waited for; matrix products, arithmetic and copies ran while one was open for 1% of the time, Pallas kernels for 13%

profile of v2, /device:TPU:0, one launch (start us, length us, event | category | flops | bytes accessed | tf_op | source)
XLA Modules:
  0.0 115.8 jit_solution(11665856355526027077)
XLA Ops:
  0.7 2.1 %collective-permute-start.1 = (f32[1,32,512]{2,1,0:T(8,128)}, f32[1,32,512]{2,1,0:T(8,128)S(1)}, u32[]{:S(2)}, u32[]{:S(2)}) collective-permute-start(f32[1,32,512]{2,1,0:T(8,128)} %given_in_ref.1), channel_id=1, source_target_pairs={{0,32},{16,48},{32,0},{48,16},{64,96},{80,112},{96,64},{112,80},{1... | collective-permute-start | bytes 196616 | tf_op jit(solution)/shard_map/ppermute | solution.py:500
  7.1 3.3 %collective-permute-start.3 = (f32[4,32,512]{2,1,0:T(8,128)S(1)}, f32[4,32,512]{2,1,0:T(8,128)S(1)}, u32[]{:S(2)}, u32[]{:S(2)}) collective-permute-start(f32[4,32,512]{2,1,0:T(8,128)S(1)} %constant_dynamic-update-slice_fusion.near_ref), channel_id=1, source_target_pairs={{0,96},{16,112},{32,64},{48,80},{64,32},{80,48},{96,0},{112,16},{1... | collective-permute-start | bytes 786440 | tf_op jit(solution)/shard_map/ppermute | solution.py:500
  10.5 5.4 %forward.2 = (f32[3,32,512]{2,1,0:T(8,128)S(1)}, f32[3,512]{1,0:T(4,128)S(1)}, bf16[3,6,64,4096]{3,2,1,0:T(8,128)(2,1)S(1)}, bf16[3,16,4096]{2,1,0:T(8,128)(2,1)...) custom-call(s32[8]{0:T(128)S(1)} %stack.26.brick_ref.info_ref, ...), custom_call_target="tpu_custom_call" | custom-call | flops 750000000 | bytes 12000000 | tf_op jit(solution)/shard_map/forward/pallas_call | solution.py:389
  15.9 8.6 %forward.3 = (f32[5,32,512]{2,1,0:T(8,128)S(1)}, f32[5,512]{1,0:T(8,128)S(1)}, bf16[5,6,64,4096]{3,2,1,0:T(8,128)(2,1)S(1)}, bf16[5,16,4096]{2,1,0:T(8,128)(2,1)...) custom-call(s32[8]{0:T(128)S(1)} %stack.26.brick_ref.info_ref, ...), custom_call_target="tpu_custom_call" | custom-call | flops 1250000000 | bytes 20000000 | tf_op jit(solution)/shard_map/forward/pallas_call | solution.py:389
  30.0 4.6 %collective-permute-done.7.got_ref = f32[2,8,512]{2,1,0:T(8,128)S(1)} collective-permute-done((f32[2,8,512]{2,1,0:T(8,128)S(1)}, f32[2,8,512]{2,1,0:T(8,128)S(1)}, u32[]{:S(2)}, u32[]{:S(2)}) %collective-permute-start.7) | collective-permute-done | bytes 32800 | tf_op jit(solution)/shard_map/ppermute | solution.py:500
  35.2 5.8 %backward.3 = (f32[2,2,3,2,64,128]{5,4,3,2,1,0:T(8,128)S(1)}, f32[1,32,512]{2,1,0:T(8,128)S(1)}) custom-call(s32[8]{0:T(128)S(1)} %stack.26.brick_ref.info_ref, s32[8,4096]{1,0:T(8,128)S(1)} %get-tuple-element.48.samples_ref, f32[4,32,512]{2,1,0:T(8,128)S(1)} %constant_dynamic-update-slice_fusion.near_ref, f32[4,32,512]{2,1,0:T(8,128)S(1)} %collective-permute-done.3.far_ref, ...), custom_call_target="tpu_custom_call" | custom-call | flops 1500000000 | bytes 13500000 | tf_op jit(solution)/shard_map/backward/pallas_call | solution.py:436
  41.0 5.8 %backward.4 = (f32[2,2,3,2,64,128]{5,4,3,2,1,0:T(8,128)S(1)}, f32[1,32,512]{2,1,0:T(8,128)S(1)}) custom-call(s32[8]{0:T(128)S(1)} %stack.26.brick_ref.info_ref, s32[8,4096]{1,0:T(8,128)S(1)} %get-tuple-element.48.samples_ref, f32[4,32,512]{2,1,0:T(8,128)S(1)} %constant_dynamic-update-slice_fusion.near_ref, f32[4,32,512]{2,1,0:T(8,128)S(1)} %collective-permute-done.3.far_ref, ...), custom_call_target="tpu_custom_call" | custom-call | flops 1500000000 | bytes 13500000 | tf_op jit(solution)/shard_map/backward/pallas_call | solution.py:436
  46.8 4.1 %backward.5 = (f32[2,2,2,2,64,128]{5,4,3,2,1,0:T(8,128)S(1)}, f32[1,32,512]{2,1,0:T(8,128)S(1)}) custom-call(s32[8]{0:T(128)S(1)} %stack.26.brick_ref.info_ref, s32[8,4096]{1,0:T(8,128)S(1)} %get-tuple-element.48.samples_ref, f32[4,32,512]{2,1,0:T(8,128)S(1)} %constant_dynamic-update-slice_fusion.near_ref, f32[4,32,512]{2,1,0:T(8,128)S(1)} %collective-permute-done.3.far_ref, ...), custom_call_target="tpu_custom_call" | custom-call | flops 1000000000 | bytes 9000000 | tf_op jit(solution)/shard_map/backward/pallas_call | solution.py:436
  54.4 2.2 %collective-permute-start.17 = (f32[2,3,2,64,128]{4,3,2,1,0:T(8,128)S(1)}, f32[2,3,2,64,128]{4,3,2,1,0:T(8,128)S(1)}, u32[]{:S(2)}, u32[]{:S(2)}) collective-permute-start(f32[2,3,2,64,128]{4,3,2,1,0:T(8,128)S(1)} %slice_bitcast_fusion), channel_id=1, source_target_pairs={{0,3},{16,17},{32,35},{48,49},{64,67},{80,81},{96,99},{112,113},{1... | collective-permute-start | bytes 1179656 | tf_op jit(solution)/shard_map/ppermute | solution.py:516
  58.5 2.7 %collective-permute-start.8 = (f32[4,32,512]{2,1,0:T(8,128)S(1)}, f32[4,32,512]{2,1,0:T(8,128)S(1)}, u32[]{:S(2)}, u32[]{:S(2)}) collective-permute-start(f32[4,32,512]{2,1,0:T(8,128)S(1)} %get-tuple-element.60), channel_id=1, source_target_pairs={{0,96},{16,112},{32,64},{48,80},{64,32},{80,48},{96,0},{112,16},{1... | collective-permute-start | bytes 786440 | tf_op jit(solution)/shard_map/ppermute | solution.py:500
  64.0 4.5 %collective-permute-done.8 = f32[4,32,512]{2,1,0:T(8,128)S(1)} collective-permute-done((f32[4,32,512]{2,1,0:T(8,128)S(1)}, f32[4,32,512]{2,1,0:T(8,128)S(1)}, u32[]{:S(2)}, u32[]{:S(2)}) %collective-permute-start.8) | collective-permute-done | bytes 262176 | tf_op jit(solution)/shard_map/ppermute | solution.py:500
  68.7 3.1 %collective-permute-start.18 = (f32[3,2,64,128]{3,2,1,0:T(8,128)S(1)}, f32[3,2,64,128]{3,2,1,0:T(8,128)S(1)}, u32[]{:S(2)}, u32[]{:S(2)}) collective-permute-start(f32[3,2,64,128]{3,2,1,0:T(8,128)S(1)} %slice_bitcast_fusion.3), channel_id=1, source_target_pairs={{0,12},{16,20},{32,44},{48,52},{64,76},{80,84},{96,108},{112,116},... | collective-permute-start | bytes 589832 | tf_op jit(solution)/shard_map/ppermute | solution.py:516
  71.9 2.2 %collective-permute-start.29 = (f32[360,128]{1,0:T(8,128)S(1)}, f32[360,128]{1,0:T(8,128)S(1)}, u32[]{:S(2)}, u32[]{:S(2)}) collective-permute-start(f32[360,128]{1,0:T(8,128)S(1)} %fusion.2), channel_id=1, source_target_pairs={{0,3},{16,17},{32,35},{48,49},{64,67},{80,81},{96,99},{112,113},{1... | collective-permute-start | bytes 552968 | tf_op jit(solution)/shard_map/ppermute | solution.py:516
  74.4 4.4 %collective-permute-done.29 = f32[360,128]{1,0:T(8,128)S(1)} collective-permute-done((f32[360,128]{1,0:T(8,128)S(1)}, f32[360,128]{1,0:T(8,128)S(1)}, u32[]{:S(2)}, u32[]{:S(2)}) %collective-permute-start.29) | collective-permute-done | bytes 184352 | tf_op jit(solution)/shard_map/ppermute | solution.py:516
  79.2 2.7 %collective-permute-done.12 = f32[3,2,64,128]{3,2,1,0:T(8,128)S(1)} collective-permute-done((f32[3,2,64,128]{3,2,1,0:T(8,128)S(1)}, f32[3,2,64,128]{3,2,1,0:T(8,128)S(1)}, u32[]{:S(2)}, u32[]{:S(2)}) %collective-permute-start.12) | collective-permute-done | bytes 196640 | tf_op jit(solution)/shard_map/ppermute | solution.py:516
  82.6 3.0 %collective-permute-done.30 = f32[360,128]{1,0:T(8,128)S(1)} collective-permute-done((f32[360,128]{1,0:T(8,128)S(1)}, f32[360,128]{1,0:T(8,128)S(1)}, u32[]{:S(2)}, u32[]{:S(2)}) %collective-permute-start.30) | collective-permute-done | bytes 184352 | tf_op jit(solution)/shard_map/ppermute | solution.py:516
  85.8 2.1 %collective-permute-start.20 = (f32[384,128]{1,0:T(8,128)S(1)}, f32[384,128]{1,0:T(8,128)S(1)}, u32[]{:S(2)}, u32[]{:S(2)}) collective-permute-start(f32[384,128]{1,0:T(8,128)S(1)} %bitcast_add_fusion.3), channel_id=1, source_target_pairs={{0,4},{16,28},{32,36},{48,60},{64,68},{80,92},{96,100},{112,124},{... | collective-permute-start | bytes 589832 | tf_op jit(solution)/shard_map/ppermute | solution.py:516
  89.4 5.7 %collective-permute-done.20 = f32[384,128]{1,0:T(8,128)S(1)} collective-permute-done((f32[384,128]{1,0:T(8,128)S(1)}, f32[384,128]{1,0:T(8,128)S(1)}, u32[]{:S(2)}, u32[]{:S(2)}) %collective-permute-start.20) | collective-permute-done | bytes 196640 | tf_op jit(solution)/shard_map/ppermute | solution.py:516
  95.4 2.2 %collective-permute-done.14 = f32[384,128]{1,0:T(8,128)S(1)} collective-permute-done((f32[384,128]{1,0:T(8,128)S(1)}, f32[384,128]{1,0:T(8,128)S(1)}, u32[]{:S(2)}, u32[]{:S(2)}) %collective-permute-start.14) | collective-permute-done | bytes 196640 | tf_op jit(solution)/shard_map/ppermute | solution.py:516
  97.9 4.2 %collective-permute-done.21.refs_4_ = f32[384,128]{1,0:T(8,128)S(1)} collective-permute-done((f32[384,128]{1,0:T(8,128)S(1)}, f32[384,128]{1,0:T(8,128)S(1)}, u32[]{:S(2)}, u32[]{:S(2)}) %collective-permute-start.21) | collective-permute-done | bytes 196640 | tf_op jit(solution)/shard_map/ppermute | solution.py:516
  102.1 3.7 %collective-permute-start.22 = (f32[768,128]{1,0:T(8,128)S(1)}, f32[768,128]{1,0:T(8,128)S(1)}, u32[]{:S(2)}, u32[]{:S(2)}) collective-permute-start(f32[768,128]{1,0:T(8,128)S(1)} %pad_maximum_fusion.1), channel_id=1, source_target_pairs={{0,3},{16,17},{32,35},{48,49},{64,67},{80,81},{96,99},{112,113},{1... | collective-permute-start | bytes 1179656 | tf_op jit(solution)/shard_map/ppermute | solution.py:516
  107.9 3.6 %collective-permute-done.22.refs_5_ = f32[768,128]{1,0:T(8,128)S(1)} collective-permute-done((f32[768,128]{1,0:T(8,128)S(1)}, f32[768,128]{1,0:T(8,128)S(1)}, u32[]{:S(2)}, u32[]{:S(2)}) %collective-permute-start.22) | collective-permute-done | bytes 393248 | tf_op jit(solution)/shard_map/ppermute | solution.py:516
  111.5 2.1 %collective-permute-done.16.refs_2_ = f32[768,128]{1,0:T(8,128)S(1)} collective-permute-done((f32[768,128]{1,0:T(8,128)S(1)}, f32[768,128]{1,0:T(8,128)S(1)}, u32[]{:S(2)}, u32[]{:S(2)}) %collective-permute-start.16) | collective-permute-done | bytes 393248 | tf_op jit(solution)/shard_map/ppermute | solution.py:516
  113.6 2.2 %finish.1 = (f32[1,16,32768]{2,1,0:T(8,128)}, f32[16,64]{1,0:T(8,128)}, f32[64,64]{1,0:T(8,128)}, f32[64,64]{1,0:T(8,128)}, f32[33,64]{1,0:T(8,128)}) custom-call(s32[8]{0:T(128)S(1)} %stack.26.brick_ref.info_ref, f32[384,128]{1,0:T(8,128)S(1)} %add.66.refs_0_, f32[384,128]{1,0:T(8,128)S(1)} %collective-permute-done.15.refs_1_, ...), custom_call_target="tpu_custom_call" | custom-call | tf_op jit(solution)/shard_map/finish/pallas_call | solution.py:483
  (91 shorter events, 24.0 us)
Async XLA Ops:
  7.1 17.3 %collective-permute-start.3 = (f32[4,32,512]{2,1,0:T(8,128)S(1)}, f32[4,32,512]{2,1,0:T(8,128)S(1)}, u32[]{:S(2)}, u32[]{:S(2)}) collective-permute-start(f32[4,32,512]{2,1,0:T(8,128)S(1)} %constant_dynamic-update-slice_fusion.near_ref), channel_id=1, source_target_pairs={{0,96},{16,112},{32,64},{48,80},{64,32},{80,48},{96,0},{112,16},{1... | collective-permute-start | bytes 786440 | tf_op jit(solution)/shard_map/ppermute | solution.py:500
  50.8 5.7 %collective-permute-start.25 = (f32[1,32,512]{2,1,0:T(8,128)S(1)}, f32[1,32,512]{2,1,0:T(8,128)S(1)}, u32[]{:S(2)}, u32[]{:S(2)}) collective-permute-start(f32[1,32,512]{2,1,0:T(8,128)S(1)} %get-tuple-element.80), channel_id=1, source_target_pairs={{0,16},{16,0},{32,48},{48,32},{64,80},{80,64},{96,112},{112,96},{1... | collective-permute-start | bytes 196616 | tf_op jit(solution)/shard_map/ppermute | solution.py:500
  50.9 5.7 %collective-permute-start.26 = (f32[1,32,512]{2,1,0:T(8,128)S(1)}, f32[1,32,512]{2,1,0:T(8,128)S(1)}, u32[]{:S(2)}, u32[]{:S(2)}) collective-permute-start(f32[1,32,512]{2,1,0:T(8,128)S(1)} %get-tuple-element.80), channel_id=1, source_target_pairs={{0,32},{16,48},{32,0},{48,16},{64,96},{80,112},{96,64},{112,80},{1... | collective-permute-start | bytes 196616 | tf_op jit(solution)/shard_map/ppermute | solution.py:500
  52.8 9.5 %collective-permute-start.23 = (f32[2,2,2,64,128]{4,3,2,1,0:T(8,128)S(1)}, f32[2,2,2,64,128]{4,3,2,1,0:T(8,128)S(1)}, u32[]{:S(2)}, u32[]{:S(2)}) collective-permute-start(f32[2,2,2,64,128]{4,3,2,1,0:T(8,128)S(1)} %slice_bitcast_fusion.2), channel_id=1, source_target_pairs={{0,1},{16,19},{32,33},{48,51},{64,65},{80,83},{96,97},{112,115},{1... | collective-permute-start | bytes 786440 | tf_op jit(solution)/shard_map/ppermute | solution.py:516
  54.4 14.2 %collective-permute-start.17 = (f32[2,3,2,64,128]{4,3,2,1,0:T(8,128)S(1)}, f32[2,3,2,64,128]{4,3,2,1,0:T(8,128)S(1)}, u32[]{:S(2)}, u32[]{:S(2)}) collective-permute-start(f32[2,3,2,64,128]{4,3,2,1,0:T(8,128)S(1)} %slice_bitcast_fusion), channel_id=1, source_target_pairs={{0,3},{16,17},{32,35},{48,49},{64,67},{80,81},{96,99},{112,113},{1... | collective-permute-start | bytes 1179656 | tf_op jit(solution)/shard_map/ppermute | solution.py:516
  56.6 5.6 %collective-permute-start.28 = (f32[1,32,512]{2,1,0:T(8,128)S(1)}, f32[1,32,512]{2,1,0:T(8,128)S(1)}, u32[]{:S(2)}, u32[]{:S(2)}) collective-permute-start(f32[1,32,512]{2,1,0:T(8,128)S(1)} %add_add_fusion), channel_id=1, source_target_pairs={{0,96},{16,112},{32,64},{48,80},{64,32},{80,48},{96,0},{112,16},{1... | collective-permute-start | bytes 196616 | tf_op jit(solution)/shard_map/ppermute | solution.py:500
  57.2 14.6 %collective-permute-start.11 = (f32[2,3,2,64,128]{4,3,2,1,0:T(8,128)S(1)}, f32[2,3,2,64,128]{4,3,2,1,0:T(8,128)S(1)}, u32[]{:S(2)}, u32[]{:S(2)}) collective-permute-start(f32[2,3,2,64,128]{4,3,2,1,0:T(8,128)S(1)} %slice_bitcast_fusion.1), channel_id=1, source_target_pairs={{0,1},{16,19},{32,33},{48,51},{64,65},{80,83},{96,97},{112,115},{1... | collective-permute-start | bytes 1179656 | tf_op jit(solution)/shard_map/ppermute | solution.py:516
  58.5 10.0 %collective-permute-start.8 = (f32[4,32,512]{2,1,0:T(8,128)S(1)}, f32[4,32,512]{2,1,0:T(8,128)S(1)}, u32[]{:S(2)}, u32[]{:S(2)}) collective-permute-start(f32[4,32,512]{2,1,0:T(8,128)S(1)} %get-tuple-element.60), channel_id=1, source_target_pairs={{0,96},{16,112},{32,64},{48,80},{64,32},{80,48},{96,0},{112,16},{1... | collective-permute-start | bytes 786440 | tf_op jit(solution)/shard_map/ppermute | solution.py:500
  62.3 9.5 %collective-permute-start.24 = (f32[2,2,64,128]{3,2,1,0:T(8,128)S(1)}, f32[2,2,64,128]{3,2,1,0:T(8,128)S(1)}, u32[]{:S(2)}, u32[]{:S(2)}) collective-permute-start(f32[2,2,64,128]{3,2,1,0:T(8,128)S(1)} %slice_bitcast_fusion.7), channel_id=1, source_target_pairs={{0,4},{16,28},{32,36},{48,60},{64,68},{80,92},{96,100},{112,124},{... | collective-permute-start | bytes 393224 | tf_op jit(solution)/shard_map/ppermute | solution.py:516
  68.6 37.3 %collective-permute-start.9 = (f32[2,32,512]{2,1,0:T(8,128)S(1)}, f32[2,32,512]{2,1,0:T(8,128)S(1)}, u32[]{:S(2)}, u32[]{:S(2)}) collective-permute-start(f32[2,32,512]{2,1,0:T(8,128)S(1)} %slice.101), channel_id=1, source_target_pairs={{0,32},{16,48},{32,0},{48,16},{64,96},{80,112},{96,64},{112,80},{1... | collective-permute-start | bytes 393224 | tf_op jit(solution)/shard_map/ppermute | solution.py:500
  68.7 10.4 %collective-permute-start.18 = (f32[3,2,64,128]{3,2,1,0:T(8,128)S(1)}, f32[3,2,64,128]{3,2,1,0:T(8,128)S(1)}, u32[]{:S(2)}, u32[]{:S(2)}) collective-permute-start(f32[3,2,64,128]{3,2,1,0:T(8,128)S(1)} %slice_bitcast_fusion.3), channel_id=1, source_target_pairs={{0,12},{16,20},{32,44},{48,52},{64,76},{80,84},{96,108},{112,116},... | collective-permute-start | bytes 589832 | tf_op jit(solution)/shard_map/ppermute | solution.py:516
  71.9 6.8 %collective-permute-start.29 = (f32[360,128]{1,0:T(8,128)S(1)}, f32[360,128]{1,0:T(8,128)S(1)}, u32[]{:S(2)}, u32[]{:S(2)}) collective-permute-start(f32[360,128]{1,0:T(8,128)S(1)} %fusion.2), channel_id=1, source_target_pairs={{0,3},{16,17},{32,35},{48,49},{64,67},{80,81},{96,99},{112,113},{1... | collective-permute-start | bytes 552968 | tf_op jit(solution)/shard_map/ppermute | solution.py:516
  74.2 7.7 %collective-permute-start.12 = (f32[3,2,64,128]{3,2,1,0:T(8,128)S(1)}, f32[3,2,64,128]{3,2,1,0:T(8,128)S(1)}, u32[]{:S(2)}, u32[]{:S(2)}) collective-permute-start(f32[3,2,64,128]{3,2,1,0:T(8,128)S(1)} %slice_bitcast_fusion.5), channel_id=1, source_target_pairs={{0,4},{16,28},{32,36},{48,60},{64,68},{80,92},{96,100},{112,124},{... | collective-permute-start | bytes 589832 | tf_op jit(solution)/shard_map/ppermute | solution.py:516
  78.8 6.8 %collective-permute-start.30 = (f32[360,128]{1,0:T(8,128)S(1)}, f32[360,128]{1,0:T(8,128)S(1)}, u32[]{:S(2)}, u32[]{:S(2)}) collective-permute-start(f32[360,128]{1,0:T(8,128)S(1)} %add.77), channel_id=1, source_target_pairs={{0,12},{16,20},{32,44},{48,52},{64,76},{80,84},{96,108},{112,116},... | collective-permute-start | bytes 552968 | tf_op jit(solution)/shard_map/ppermute | solution.py:516
  79.1 6.6 %collective-permute-start.19 = (f32[384,128]{1,0:T(8,128)S(1)}, f32[384,128]{1,0:T(8,128)S(1)}, u32[]{:S(2)}, u32[]{:S(2)}) collective-permute-start(f32[384,128]{1,0:T(8,128)S(1)} %bitcast.53), channel_id=1, source_target_pairs={{0,1},{16,19},{32,33},{48,51},{64,65},{80,83},{96,97},{112,115},{1... | collective-permute-start | bytes 589832 | tf_op jit(solution)/shard_map/ppermute | solution.py:516
  81.9 7.0 %collective-permute-start.13 = (f32[384,128]{1,0:T(8,128)S(1)}, f32[384,128]{1,0:T(8,128)S(1)}, u32[]{:S(2)}, u32[]{:S(2)}) collective-permute-start(f32[384,128]{1,0:T(8,128)S(1)} %bitcast.54), channel_id=1, source_target_pairs={{0,3},{16,17},{32,35},{48,49},{64,67},{80,81},{96,99},{112,113},{1... | collective-permute-start | bytes 589832 | tf_op jit(solution)/shard_map/ppermute | solution.py:516
  85.7 9.7 %collective-permute-start.31 = (f32[360,128]{1,0:T(8,128)S(1)}, f32[360,128]{1,0:T(8,128)S(1)}, u32[]{:S(2)}, u32[]{:S(2)}) collective-permute-start(f32[360,128]{1,0:T(8,128)S(1)} %add.78.refs_6_), channel_id=1, source_target_pairs={{0,4},{16,28},{32,36},{48,60},{64,68},{80,92},{96,100},{112,124},{... | collective-permute-start | bytes 552968 | tf_op jit(solution)/shard_map/ppermute | solution.py:516
  85.8 9.3 %collective-permute-start.20 = (f32[384,128]{1,0:T(8,128)S(1)}, f32[384,128]{1,0:T(8,128)S(1)}, u32[]{:S(2)}, u32[]{:S(2)}) collective-permute-start(f32[384,128]{1,0:T(8,128)S(1)} %bitcast_add_fusion.3), channel_id=1, source_target_pairs={{0,4},{16,28},{32,36},{48,60},{64,68},{80,92},{96,100},{112,124},{... | collective-permute-start | bytes 589832 | tf_op jit(solution)/shard_map/ppermute | solution.py:516
  88.9 8.7 %collective-permute-start.14 = (f32[384,128]{1,0:T(8,128)S(1)}, f32[384,128]{1,0:T(8,128)S(1)}, u32[]{:S(2)}, u32[]{:S(2)}) collective-permute-start(f32[384,128]{1,0:T(8,128)S(1)} %bitcast_add_fusion.4), channel_id=1, source_target_pairs={{0,12},{16,20},{32,44},{48,52},{64,76},{80,84},{96,108},{112,116},... | collective-permute-start | bytes 589832 | tf_op jit(solution)/shard_map/ppermute | solution.py:516
  95.1 7.0 %collective-permute-start.21 = (f32[384,128]{1,0:T(8,128)S(1)}, f32[384,128]{1,0:T(8,128)S(1)}, u32[]{:S(2)}, u32[]{:S(2)}) collective-permute-start(f32[384,128]{1,0:T(8,128)S(1)} %add.70.refs_3_), channel_id=1, source_target_pairs={{0,12},{16,20},{32,44},{48,52},{64,76},{80,84},{96,108},{112,116},... | collective-permute-start | bytes 589832 | tf_op jit(solution)/shard_map/ppermute | solution.py:516
  97.6 8.1 %collective-permute-start.15 = (f32[384,128]{1,0:T(8,128)S(1)}, f32[384,128]{1,0:T(8,128)S(1)}, u32[]{:S(2)}, u32[]{:S(2)}) collective-permute-start(f32[384,128]{1,0:T(8,128)S(1)} %add.66.refs_0_), channel_id=1, source_target_pairs={{0,4},{16,28},{32,36},{48,60},{64,68},{80,92},{96,100},{112,124},{... | collective-permute-start | bytes 589832 | tf_op jit(solution)/shard_map/ppermute | solution.py:516
  97.8 10.1 %collective-permute-start.32 = (f32[616,128]{1,0:T(8,128)S(1)}, f32[616,128]{1,0:T(8,128)S(1)}, u32[]{:S(2)}, u32[]{:S(2)}) collective-permute-start(f32[616,128]{1,0:T(8,128)S(1)} %pad_maximum_fusion.2), channel_id=1, source_target_pairs={{0,1},{16,19},{32,33},{48,51},{64,65},{80,83},{96,97},{112,115},{1... | collective-permute-start | bytes 946184 | tf_op jit(solution)/shard_map/ppermute | solution.py:516
  102.1 9.4 %collective-permute-start.22 = (f32[768,128]{1,0:T(8,128)S(1)}, f32[768,128]{1,0:T(8,128)S(1)}, u32[]{:S(2)}, u32[]{:S(2)}) collective-permute-start(f32[768,128]{1,0:T(8,128)S(1)} %pad_maximum_fusion.1), channel_id=1, source_target_pairs={{0,3},{16,17},{32,35},{48,49},{64,67},{80,81},{96,99},{112,113},{1... | collective-permute-start | bytes 1179656 | tf_op jit(solution)/shard_map/ppermute | solution.py:516
  105.8 7.9 %collective-permute-start.16 = (f32[768,128]{1,0:T(8,128)S(1)}, f32[768,128]{1,0:T(8,128)S(1)}, u32[]{:S(2)}, u32[]{:S(2)}) collective-permute-start(f32[768,128]{1,0:T(8,128)S(1)} %pad_maximum_fusion), channel_id=1, source_target_pairs={{0,1},{16,19},{32,33},{48,51},{64,65},{80,83},{96,97},{112,115},{1... | collective-permute-start | bytes 1179656 | tf_op jit(solution)/shard_map/ppermute | solution.py:516
  (9 other events, 35.6 us)

commit v3 on v2

--- a/solution.py
+++ b/solution.py
@@ -20,6 +20,7 @@
 FIRSTS = tuple(sum(SIZES[:c]) for c in range(len(SIZES)))
 COLOURS = len(SIZES)
 LAST = COLOURS - 1
+HALVED = (1, 2)
 SPLIT = 3
 
 
@@ -282,7 +283,7 @@
 
 
 def finish_kernel(info_ref, *refs):
-    sources, (packed_in_ref, grid_ref, one_t_ref, two_ref, three_ref, four_ref) = refs[: 3 * COLOURS], refs[3 * COLOURS :]
+    sources, (packed_in_ref, grid_ref, one_t_ref, two_ref, three_ref, four_ref) = refs[: 4 * COLOURS], refs[4 * COLOURS :]
     channels = grid_ref.shape[1]
     slab = grid_ref.shape[2] // STEPS
 
@@ -290,8 +291,8 @@
     for colour in range(COLOURS):
         rows = 2 * SIZES[colour] * unit
         for part in range(4):
-            source = sources[3 * colour + min(part, 2)]
-            skip = rows if part == 3 else 0
+            source = sources[4 * colour + part]
+            skip = rows if part == 3 and colour not in HALVED else 0
             half = jnp.bitwise_xor(info_ref[2 + colour], part // 2)
             quarter = jnp.bitwise_xor(info_ref[2 + COLOURS + colour], part % 2)
             for at in range(SIZES[colour]):
@@ -302,7 +303,7 @@
                         row = skip + (at * 2 + step) * unit + k * channels
                         span = pl.ds(pl.multiple_of(start + k * LANES, LANES), LANES)
                         grid_ref[0, :, span] = source[row : row + channels, :]
-    packed_in_ref = packed_in_ref[...] + sources[3 * LAST + 2][2 * rows :, :]
+    packed_in_ref = packed_in_ref[...] + sources[4 * LAST + 3][-104:, :]
     one_t_ref[...] = packed_in_ref[64:80, 64:128]
     two_ref[...] = packed_in_ref[0:64, 0:64]
     three_ref[...] = packed_in_ref[0:64, 64:128]
@@ -489,7 +490,7 @@
             jax.ShapeDtypeStruct((64, 64), F32),
             jax.ShapeDtypeStruct((33, 64), F32),
         ],
-        in_specs=[SMEM] + [VMEM] * (3 * COLOURS + 1),
+        in_specs=[SMEM] + [VMEM] * (4 * COLOURS + 1),
         out_specs=[VMEM] * 5,
         compiler_params=pltpu.CompilerParams(vmem_limit_bytes=14 * 2**20),
         name="finish",
@@ -566,8 +567,8 @@
     )
 
     image = image_near + swap_brick(image_far, 6)
-    image = image[:2] + swap_brick(image[2:], 2)
-    image = image[:1] + swap_brick(image[1:], 1)
+    got = [swap_brick(image[k : k + 1], k) for k in (1, 2, 3)]
+    image = image[:1] + got[0] + (got[1] + got[2])
 
     packed = jnp.zeros((1, 32, TILE), F32)
     grids = []
@@ -595,11 +596,14 @@
         for turn in (2, 3):
             part = part + view_swap(part, colour, turn)
         got = view_swap(part, colour, 1)
-        sent = jnp.concatenate([part[:rows], got[:rows]], axis=0)
+        halved = colour in HALVED
+        sent = got[:rows] if halved else jnp.concatenate([part[:rows], got[:rows]], axis=0)
         if colour == LAST:
             packed = part[rows:] + got[rows:]
             sent = jnp.concatenate([sent, packed], axis=0)
-        sources += [part, got, view_swap(sent, colour, 0)]
+        far = view_swap(sent, colour, 0)
+        first = view_swap(part[:rows], colour, 0) if halved else far
+        sources += [part, got, first, far]
 
     channels = latent_grid.shape[1]
     grid, one_t, two, three, four = run_finish(info, sources, packed, channels, voxels)

time: 116 us -> 120 us (1.034)
  starting transfers between devices: 33.5 us -> 45 us
  waiting for transfers between devices: 44.6 us -> 37.8 us
    ppermute x18 -> x20, starting transfers between devices: 20 us -> 29.4 us  [view_swap(): return lax.ppermute(array, ('brick', 'view'), pairs)]
    ppermute x18 -> x20, waiting for transfers between devices: 29 us -> 23.3 us  [view_swap(): return lax.ppermute(array, ('brick', 'view'), pairs)]
    ppermute x15 -> x16, starting transfers between devices: 13.5 us -> 15.6 us  [swap_brick(): return lax.ppermute(array, 'brick', [(i, i ^ flip) for i in range(8)])]
    ppermute x15 -> x16, waiting for transfers between devices: 15.7 us -> 14.4 us  [swap_brick(): return lax.ppermute(array, 'brick', [(i, i ^ flip) for i in range(8)])]
  transfers between devices with their start and end apart: 33 -> 36, of which waited for: 16 -> 14; matrix products, arithmetic and copies ran while one was open for 1% -> 1% of each run, Pallas kernels for 13% -> 13%
where the time goes in v3:
time: 120 us
  starting transfers between devices  45 us (38%)
  waiting for transfers between devices  37.8 us (31%)
  Pallas kernels  34.5 us (29%)
  between operations  1.66 us (1%)
    ppermute x20, starting transfers between devices, view_swap(): return lax.ppermute(array, ('brick', 'view'), pairs)  29.4 us
    ppermute x20, waiting for transfers between devices, view_swap(): return lax.ppermute(array, ('brick', 'view'), pairs)  23.3 us
    ppermute x16, starting transfers between devices, swap_brick(): return lax.ppermute(array, 'brick', [(i, i ^ flip) for i in range(8)])  15.6 us
    pallas_call x3, Pallas kernels, run_backward(): pl.pallas_call(functools.partial(backward_kernel, colour), out_shape=[jax...  15.6 us
    ppermute x16, waiting for transfers between devices, swap_brick(): return lax.ppermute(array, 'brick', [(i, i ^ flip) for i in range(8)])  14.4 us
    pallas_call x2, Pallas kernels, run_forward(): pl.pallas_call(functools.partial(forward_kernel, first), out_shape=shapes...  13.9 us
  transfers between devices with their start and end apart: 36, of which 14 were waited for; matrix products, arithmetic and copies ran while one was open for 1% of the time, Pallas kernels for 13%

profile of v3, /device:TPU:0, one launch (start us, length us, event | category | flops | bytes accessed | tf_op | source)
XLA Modules:
  0.0 120.3 jit_solution(241697864183480638)
XLA Ops:
  0.7 2.1 %collective-permute-start.1 = (f32[1,32,512]{2,1,0:T(8,128)}, f32[1,32,512]{2,1,0:T(8,128)S(1)}, u32[]{:S(2)}, u32[]{:S(2)}) collective-permute-start(f32[1,32,512]{2,1,0:T(8,128)} %given_in_ref.1), channel_id=1, source_target_pairs={{0,32},{16,48},{32,0},{48,16},{64,96},{80,112},{96,64},{112,80},{1... | collective-permute-start | bytes 196616 | tf_op jit(solution)/shard_map/ppermute | solution.py:501
  7.1 3.3 %collective-permute-start.3 = (f32[4,32,512]{2,1,0:T(8,128)S(1)}, f32[4,32,512]{2,1,0:T(8,128)S(1)}, u32[]{:S(2)}, u32[]{:S(2)}) collective-permute-start(f32[4,32,512]{2,1,0:T(8,128)S(1)} %constant_dynamic-update-slice_fusion.near_ref), channel_id=1, source_target_pairs={{0,96},{16,112},{32,64},{48,80},{64,32},{80,48},{96,0},{112,16},{1... | collective-permute-start | bytes 786440 | tf_op jit(solution)/shard_map/ppermute | solution.py:501
  10.5 5.4 %forward.2 = (f32[3,32,512]{2,1,0:T(8,128)S(1)}, f32[3,512]{1,0:T(4,128)S(1)}, bf16[3,6,64,4096]{3,2,1,0:T(8,128)(2,1)S(1)}, bf16[3,16,4096]{2,1,0:T(8,128)(2,1)...) custom-call(s32[8]{0:T(128)S(1)} %stack.26.brick_ref.info_ref, ...), custom_call_target="tpu_custom_call" | custom-call | flops 750000000 | bytes 12000000 | tf_op jit(solution)/shard_map/forward/pallas_call | solution.py:390
  15.9 8.6 %forward.3 = (f32[5,32,512]{2,1,0:T(8,128)S(1)}, f32[5,512]{1,0:T(8,128)S(1)}, bf16[5,6,64,4096]{3,2,1,0:T(8,128)(2,1)S(1)}, bf16[5,16,4096]{2,1,0:T(8,128)(2,1)...) custom-call(s32[8]{0:T(128)S(1)} %stack.26.brick_ref.info_ref, ...), custom_call_target="tpu_custom_call" | custom-call | flops 1250000000 | bytes 20000000 | tf_op jit(solution)/shard_map/forward/pallas_call | solution.py:390
  30.0 4.6 %collective-permute-done.7.got_ref = f32[2,8,512]{2,1,0:T(8,128)S(1)} collective-permute-done((f32[2,8,512]{2,1,0:T(8,128)S(1)}, f32[2,8,512]{2,1,0:T(8,128)S(1)}, u32[]{:S(2)}, u32[]{:S(2)}) %collective-permute-start.7) | collective-permute-done | bytes 32800 | tf_op jit(solution)/shard_map/ppermute | solution.py:501
  35.2 5.8 %backward.3 = (f32[2,2,3,2,64,128]{5,4,3,2,1,0:T(8,128)S(1)}, f32[1,32,512]{2,1,0:T(8,128)S(1)}) custom-call(s32[8]{0:T(128)S(1)} %stack.26.brick_ref.info_ref, s32[8,4096]{1,0:T(8,128)S(1)} %get-tuple-element.48.samples_ref, f32[4,32,512]{2,1,0:T(8,128)S(1)} %constant_dynamic-update-slice_fusion.near_ref, f32[4,32,512]{2,1,0:T(8,128)S(1)} %collective-permute-done.3.far_ref, ...), custom_call_target="tpu_custom_call" | custom-call | flops 1500000000 | bytes 13500000 | tf_op jit(solution)/shard_map/backward/pallas_call | solution.py:437
  41.0 5.8 %backward.4 = (f32[2,2,3,2,64,128]{5,4,3,2,1,0:T(8,128)S(1)}, f32[1,32,512]{2,1,0:T(8,128)S(1)}) custom-call(s32[8]{0:T(128)S(1)} %stack.26.brick_ref.info_ref, s32[8,4096]{1,0:T(8,128)S(1)} %get-tuple-element.48.samples_ref, f32[4,32,512]{2,1,0:T(8,128)S(1)} %constant_dynamic-update-slice_fusion.near_ref, f32[4,32,512]{2,1,0:T(8,128)S(1)} %collective-permute-done.3.far_ref, ...), custom_call_target="tpu_custom_call" | custom-call | flops 1500000000 | bytes 13500000 | tf_op jit(solution)/shard_map/backward/pallas_call | solution.py:437
  46.8 4.0 %backward.5 = (f32[2,2,2,2,64,128]{5,4,3,2,1,0:T(8,128)S(1)}, f32[1,32,512]{2,1,0:T(8,128)S(1)}) custom-call(s32[8]{0:T(128)S(1)} %stack.26.brick_ref.info_ref, s32[8,4096]{1,0:T(8,128)S(1)} %get-tuple-element.48.samples_ref, f32[4,32,512]{2,1,0:T(8,128)S(1)} %constant_dynamic-update-slice_fusion.near_ref, f32[4,32,512]{2,1,0:T(8,128)S(1)} %collective-permute-done.3.far_ref, ...), custom_call_target="tpu_custom_call" | custom-call | flops 1000000000 | bytes 9000000 | tf_op jit(solution)/shard_map/backward/pallas_call | solution.py:437
  54.4 2.2 %collective-permute-start.18 = (f32[2,3,2,64,128]{4,3,2,1,0:T(8,128)S(1)}, f32[2,3,2,64,128]{4,3,2,1,0:T(8,128)S(1)}, u32[]{:S(2)}, u32[]{:S(2)}) collective-permute-start(f32[2,3,2,64,128]{4,3,2,1,0:T(8,128)S(1)} %slice_bitcast_fusion), channel_id=1, source_target_pairs={{0,3},{16,17},{32,35},{48,49},{64,67},{80,81},{96,99},{112,113},{1... | collective-permute-start | bytes 1179656 | tf_op jit(solution)/shard_map/ppermute | solution.py:517
  58.5 2.7 %collective-permute-start.8 = (f32[4,32,512]{2,1,0:T(8,128)S(1)}, f32[4,32,512]{2,1,0:T(8,128)S(1)}, u32[]{:S(2)}, u32[]{:S(2)}) collective-permute-start(f32[4,32,512]{2,1,0:T(8,128)S(1)} %get-tuple-element.60), channel_id=1, source_target_pairs={{0,96},{16,112},{32,64},{48,80},{64,32},{80,48},{96,0},{112,16},{1... | collective-permute-start | bytes 786440 | tf_op jit(solution)/shard_map/ppermute | solution.py:501
  64.0 4.5 %collective-permute-done.8 = f32[4,32,512]{2,1,0:T(8,128)S(1)} collective-permute-done((f32[4,32,512]{2,1,0:T(8,128)S(1)}, f32[4,32,512]{2,1,0:T(8,128)S(1)}, u32[]{:S(2)}, u32[]{:S(2)}) %collective-permute-start.8) | collective-permute-done | bytes 262176 | tf_op jit(solution)/shard_map/ppermute | solution.py:501
  70.4 2.2 %collective-permute-start.31 = (f32[360,128]{1,0:T(8,128)S(1)}, f32[360,128]{1,0:T(8,128)S(1)}, u32[]{:S(2)}, u32[]{:S(2)}) collective-permute-start(f32[360,128]{1,0:T(8,128)S(1)} %fusion.2), channel_id=1, source_target_pairs={{0,3},{16,17},{32,35},{48,49},{64,67},{80,81},{96,99},{112,113},{1... | collective-permute-start | bytes 552968 | tf_op jit(solution)/shard_map/ppermute | solution.py:517
  72.6 2.3 %collective-permute-start.19 = (f32[3,2,64,128]{3,2,1,0:T(8,128)S(1)}, f32[3,2,64,128]{3,2,1,0:T(8,128)S(1)}, u32[]{:S(2)}, u32[]{:S(2)}) collective-permute-start(f32[3,2,64,128]{3,2,1,0:T(8,128)S(1)} %slice_bitcast_fusion.3), channel_id=1, source_target_pairs={{0,12},{16,20},{32,44},{48,52},{64,76},{80,84},{96,108},{112,116},... | collective-permute-start | bytes 589832 | tf_op jit(solution)/shard_map/ppermute | solution.py:517
  74.9 2.4 %collective-permute-done.31 = f32[360,128]{1,0:T(8,128)S(1)} collective-permute-done((f32[360,128]{1,0:T(8,128)S(1)}, f32[360,128]{1,0:T(8,128)S(1)}, u32[]{:S(2)}, u32[]{:S(2)}) %collective-permute-start.31) | collective-permute-done | bytes 184352 | tf_op jit(solution)/shard_map/ppermute | solution.py:517
  77.3 2.3 %collective-permute-start.32 = (f32[360,128]{1,0:T(8,128)S(1)}, f32[360,128]{1,0:T(8,128)S(1)}, u32[]{:S(2)}, u32[]{:S(2)}) collective-permute-start(f32[360,128]{1,0:T(8,128)S(1)} %add.81), channel_id=1, source_target_pairs={{0,12},{16,20},{32,44},{48,52},{64,76},{80,84},{96,108},{112,116},... | collective-permute-start | bytes 552968 | tf_op jit(solution)/shard_map/ppermute | solution.py:517
  79.6 2.2 %collective-permute-start.14 = (f32[384,128]{1,0:T(8,128)S(1)}, f32[384,128]{1,0:T(8,128)S(1)}, u32[]{:S(2)}, u32[]{:S(2)}) collective-permute-start(f32[384,128]{1,0:T(8,128)S(1)} %bitcast.53), channel_id=1, source_target_pairs={{0,3},{16,17},{32,35},{48,49},{64,67},{80,81},{96,99},{112,113},{1... | collective-permute-start | bytes 589832 | tf_op jit(solution)/shard_map/ppermute | solution.py:517
  81.9 2.2 %collective-permute-done.32 = f32[360,128]{1,0:T(8,128)S(1)} collective-permute-done((f32[360,128]{1,0:T(8,128)S(1)}, f32[360,128]{1,0:T(8,128)S(1)}, u32[]{:S(2)}, u32[]{:S(2)}) %collective-permute-start.32) | collective-permute-done | bytes 184352 | tf_op jit(solution)/shard_map/ppermute | solution.py:517
  88.8 5.9 %collective-permute-done.15 = f32[384,128]{1,0:T(8,128)S(1)} collective-permute-done((f32[384,128]{1,0:T(8,128)S(1)}, f32[384,128]{1,0:T(8,128)S(1)}, u32[]{:S(2)}, u32[]{:S(2)}) %collective-permute-start.15) | collective-permute-done | bytes 196640 | tf_op jit(solution)/shard_map/ppermute | solution.py:517
  95.3 2.1 %collective-permute-start.9 = (f32[1,32,512]{2,1,0:T(8,128)S(1)}, f32[1,32,512]{2,1,0:T(8,128)S(1)}, u32[]{:S(2)}, u32[]{:S(2)}) collective-permute-start(f32[1,32,512]{2,1,0:T(8,128)S(1)} %get-tuple-element.88), channel_id=1, source_target_pairs={{0,16},{16,0},{32,48},{48,32},{64,80},{80,64},{96,112},{112,96},{1... | collective-permute-start | bytes 196616 | tf_op jit(solution)/shard_map/ppermute | solution.py:501
  97.4 3.2 %collective-permute-done.16.refs_1_ = f32[384,128]{1,0:T(8,128)S(1)} collective-permute-done((f32[384,128]{1,0:T(8,128)S(1)}, f32[384,128]{1,0:T(8,128)S(1)}, u32[]{:S(2)}, u32[]{:S(2)}) %collective-permute-start.16) | collective-permute-done | bytes 196640 | tf_op jit(solution)/shard_map/ppermute | solution.py:517
  100.7 2.3 %collective-permute-start.22 = (f32[384,128]{1,0:T(8,128)S(1)}, f32[384,128]{1,0:T(8,128)S(1)}, u32[]{:S(2)}, u32[]{:S(2)}) collective-permute-start(f32[384,128]{1,0:T(8,128)S(1)} %add.74.refs_4_), channel_id=1, source_target_pairs={{0,12},{16,20},{32,44},{48,52},{64,76},{80,84},{96,108},{112,116},... | collective-permute-start | bytes 589832 | tf_op jit(solution)/shard_map/ppermute | solution.py:517
  107.5 2.2 %collective-permute-start.24 = (f32[384,128]{1,0:T(8,128)S(1)}, f32[384,128]{1,0:T(8,128)S(1)}, u32[]{:S(2)}, u32[]{:S(2)}) collective-permute-start(f32[384,128]{1,0:T(8,128)S(1)} %collective-permute-done.22.refs_5_), channel_id=1, source_target_pairs={{0,3},{16,17},{32,35},{48,49},{64,67},{80,81},{96,99},{112,113},{1... | collective-permute-start | bytes 589832 | tf_op jit(solution)/shard_map/ppermute | solution.py:517
  110.3 5.8 %collective-permute-done.34.refs_10_ = f32[256,128]{1,0:T(8,128)S(1)} collective-permute-done((f32[256,128]{1,0:T(8,128)S(1)}, f32[256,128]{1,0:T(8,128)S(1)}, u32[]{:S(2)}, u32[]{:S(2)}) %collective-permute-start.34) | collective-permute-done | bytes 131104 | tf_op jit(solution)/shard_map/ppermute | solution.py:517
  118.1 2.2 %finish.1 = (f32[1,16,32768]{2,1,0:T(8,128)}, f32[16,64]{1,0:T(8,128)}, f32[64,64]{1,0:T(8,128)}, f32[64,64]{1,0:T(8,128)}, f32[33,64]{1,0:T(8,128)}) custom-call(s32[8]{0:T(128)S(1)} %stack.26.brick_ref.info_ref, f32[384,128]{1,0:T(8,128)S(1)} %add.70.refs_0_, f32[384,128]{1,0:T(8,128)S(1)} %collective-permute-done.16.refs_1_, ...), custom_call_target="tpu_custom_call" | custom-call | tf_op jit(solution)/shard_map/finish/pallas_call | solution.py:484
  (94 shorter events, 32.7 us)
Async XLA Ops:
  7.1 17.3 %collective-permute-start.3 = (f32[4,32,512]{2,1,0:T(8,128)S(1)}, f32[4,32,512]{2,1,0:T(8,128)S(1)}, u32[]{:S(2)}, u32[]{:S(2)}) collective-permute-start(f32[4,32,512]{2,1,0:T(8,128)S(1)} %constant_dynamic-update-slice_fusion.near_ref), channel_id=1, source_target_pairs={{0,96},{16,112},{32,64},{48,80},{64,32},{80,48},{96,0},{112,16},{1... | collective-permute-start | bytes 786440 | tf_op jit(solution)/shard_map/ppermute | solution.py:501
  52.8 9.5 %collective-permute-start.25 = (f32[2,2,2,64,128]{4,3,2,1,0:T(8,128)S(1)}, f32[2,2,2,64,128]{4,3,2,1,0:T(8,128)S(1)}, u32[]{:S(2)}, u32[]{:S(2)}) collective-permute-start(f32[2,2,2,64,128]{4,3,2,1,0:T(8,128)S(1)} %slice_bitcast_fusion.2), channel_id=1, source_target_pairs={{0,1},{16,19},{32,33},{48,51},{64,65},{80,83},{96,97},{112,115},{1... | collective-permute-start | bytes 786440 | tf_op jit(solution)/shard_map/ppermute | solution.py:517
  54.4 15.9 %collective-permute-start.18 = (f32[2,3,2,64,128]{4,3,2,1,0:T(8,128)S(1)}, f32[2,3,2,64,128]{4,3,2,1,0:T(8,128)S(1)}, u32[]{:S(2)}, u32[]{:S(2)}) collective-permute-start(f32[2,3,2,64,128]{4,3,2,1,0:T(8,128)S(1)} %slice_bitcast_fusion), channel_id=1, source_target_pairs={{0,3},{16,17},{32,35},{48,49},{64,67},{80,81},{96,99},{112,113},{1... | collective-permute-start | bytes 1179656 | tf_op jit(solution)/shard_map/ppermute | solution.py:517
  57.2 11.3 %collective-permute-start.12 = (f32[2,3,2,64,128]{4,3,2,1,0:T(8,128)S(1)}, f32[2,3,2,64,128]{4,3,2,1,0:T(8,128)S(1)}, u32[]{:S(2)}, u32[]{:S(2)}) collective-permute-start(f32[2,3,2,64,128]{4,3,2,1,0:T(8,128)S(1)} %slice_bitcast_fusion.1), channel_id=1, source_target_pairs={{0,1},{16,19},{32,33},{48,51},{64,65},{80,83},{96,97},{112,115},{1... | collective-permute-start | bytes 1179656 | tf_op jit(solution)/shard_map/ppermute | solution.py:517
  58.5 10.0 %collective-permute-start.8 = (f32[4,32,512]{2,1,0:T(8,128)S(1)}, f32[4,32,512]{2,1,0:T(8,128)S(1)}, u32[]{:S(2)}, u32[]{:S(2)}) collective-permute-start(f32[4,32,512]{2,1,0:T(8,128)S(1)} %get-tuple-element.60), channel_id=1, source_target_pairs={{0,96},{16,112},{32,64},{48,80},{64,32},{80,48},{96,0},{112,16},{1... | collective-permute-start | bytes 786440 | tf_op jit(solution)/shard_map/ppermute | solution.py:501
  62.3 8.0 %collective-permute-start.26 = (f32[2,2,64,128]{3,2,1,0:T(8,128)S(1)}, f32[2,2,64,128]{3,2,1,0:T(8,128)S(1)}, u32[]{:S(2)}, u32[]{:S(2)}) collective-permute-start(f32[2,2,64,128]{3,2,1,0:T(8,128)S(1)} %slice_bitcast_fusion.7), channel_id=1, source_target_pairs={{0,4},{16,28},{32,36},{48,60},{64,68},{80,92},{96,100},{112,124},{... | collective-permute-start | bytes 393224 | tf_op jit(solution)/shard_map/ppermute | solution.py:517
  68.6 10.9 %collective-permute-start.13 = (f32[3,2,64,128]{3,2,1,0:T(8,128)S(1)}, f32[3,2,64,128]{3,2,1,0:T(8,128)S(1)}, u32[]{:S(2)}, u32[]{:S(2)}) collective-permute-start(f32[3,2,64,128]{3,2,1,0:T(8,128)S(1)} %slice_bitcast_fusion.5), channel_id=1, source_target_pairs={{0,4},{16,28},{32,36},{48,60},{64,68},{80,92},{96,100},{112,124},{... | collective-permute-start | bytes 589832 | tf_op jit(solution)/shard_map/ppermute | solution.py:517
  70.4 6.8 %collective-permute-start.31 = (f32[360,128]{1,0:T(8,128)S(1)}, f32[360,128]{1,0:T(8,128)S(1)}, u32[]{:S(2)}, u32[]{:S(2)}) collective-permute-start(f32[360,128]{1,0:T(8,128)S(1)} %fusion.2), channel_id=1, source_target_pairs={{0,3},{16,17},{32,35},{48,49},{64,67},{80,81},{96,99},{112,113},{1... | collective-permute-start | bytes 552968 | tf_op jit(solution)/shard_map/ppermute | solution.py:517
  72.6 9.1 %collective-permute-start.19 = (f32[3,2,64,128]{3,2,1,0:T(8,128)S(1)}, f32[3,2,64,128]{3,2,1,0:T(8,128)S(1)}, u32[]{:S(2)}, u32[]{:S(2)}) collective-permute-start(f32[3,2,64,128]{3,2,1,0:T(8,128)S(1)} %slice_bitcast_fusion.3), channel_id=1, source_target_pairs={{0,12},{16,20},{32,44},{48,52},{64,76},{80,84},{96,108},{112,116},... | collective-permute-start | bytes 589832 | tf_op jit(solution)/shard_map/ppermute | solution.py:517
  77.3 6.8 %collective-permute-start.32 = (f32[360,128]{1,0:T(8,128)S(1)}, f32[360,128]{1,0:T(8,128)S(1)}, u32[]{:S(2)}, u32[]{:S(2)}) collective-permute-start(f32[360,128]{1,0:T(8,128)S(1)} %add.81), channel_id=1, source_target_pairs={{0,12},{16,20},{32,44},{48,52},{64,76},{80,84},{96,108},{112,116},... | collective-permute-start | bytes 552968 | tf_op jit(solution)/shard_map/ppermute | solution.py:517
  79.6 7.0 %collective-permute-start.14 = (f32[384,128]{1,0:T(8,128)S(1)}, f32[384,128]{1,0:T(8,128)S(1)}, u32[]{:S(2)}, u32[]{:S(2)}) collective-permute-start(f32[384,128]{1,0:T(8,128)S(1)} %bitcast.53), channel_id=1, source_target_pairs={{0,3},{16,17},{32,35},{48,49},{64,67},{80,81},{96,99},{112,113},{1... | collective-permute-start | bytes 589832 | tf_op jit(solution)/shard_map/ppermute | solution.py:517
  81.8 6.2 %collective-permute-start.20 = (f32[384,128]{1,0:T(8,128)S(1)}, f32[384,128]{1,0:T(8,128)S(1)}, u32[]{:S(2)}, u32[]{:S(2)}) collective-permute-start(f32[384,128]{1,0:T(8,128)S(1)} %bitcast.54), channel_id=1, source_target_pairs={{0,1},{16,19},{32,33},{48,51},{64,65},{80,83},{96,97},{112,115},{1... | collective-permute-start | bytes 589832 | tf_op jit(solution)/shard_map/ppermute | solution.py:517
  84.1 18.8 %collective-permute-start.33 = (f32[360,128]{1,0:T(8,128)S(1)}, f32[360,128]{1,0:T(8,128)S(1)}, u32[]{:S(2)}, u32[]{:S(2)}) collective-permute-start(f32[360,128]{1,0:T(8,128)S(1)} %add.82.refs_8_), channel_id=1, source_target_pairs={{0,4},{16,28},{32,36},{48,60},{64,68},{80,92},{96,100},{112,124},{... | collective-permute-start | bytes 552968 | tf_op jit(solution)/shard_map/ppermute | solution.py:517
  86.6 8.1 %collective-permute-start.15 = (f32[384,128]{1,0:T(8,128)S(1)}, f32[384,128]{1,0:T(8,128)S(1)}, u32[]{:S(2)}, u32[]{:S(2)}) collective-permute-start(f32[384,128]{1,0:T(8,128)S(1)} %bitcast_add_fusion.4), channel_id=1, source_target_pairs={{0,12},{16,20},{32,44},{48,52},{64,76},{80,84},{96,108},{112,116},... | collective-permute-start | bytes 589832 | tf_op jit(solution)/shard_map/ppermute | solution.py:517
  88.0 7.3 %collective-permute-start.21 = (f32[384,128]{1,0:T(8,128)S(1)}, f32[384,128]{1,0:T(8,128)S(1)}, u32[]{:S(2)}, u32[]{:S(2)}) collective-permute-start(f32[384,128]{1,0:T(8,128)S(1)} %bitcast_add_fusion.3), channel_id=1, source_target_pairs={{0,4},{16,28},{32,36},{48,60},{64,68},{80,92},{96,100},{112,124},{... | collective-permute-start | bytes 589832 | tf_op jit(solution)/shard_map/ppermute | solution.py:517
  95.1 8.0 %collective-permute-start.10 = (f32[1,32,512]{2,1,0:T(8,128)S(1)}, f32[1,32,512]{2,1,0:T(8,128)S(1)}, u32[]{:S(2)}, u32[]{:S(2)}) collective-permute-start(f32[1,32,512]{2,1,0:T(8,128)S(1)} %get-tuple-element.87), channel_id=1, source_target_pairs={{0,32},{16,48},{32,0},{48,16},{64,96},{80,112},{96,64},{112,80},{1... | collective-permute-start | bytes 196616 | tf_op jit(solution)/shard_map/ppermute | solution.py:501
  95.2 10.0 %collective-permute-start.11 = (f32[1,32,512]{2,1,0:T(8,128)S(1)}, f32[1,32,512]{2,1,0:T(8,128)S(1)}, u32[]{:S(2)}, u32[]{:S(2)}) collective-permute-start(f32[1,32,512]{2,1,0:T(8,128)S(1)} %get-tuple-element.86), channel_id=1, source_target_pairs={{0,48},{16,32},{32,16},{48,0},{64,112},{80,96},{96,80},{112,64},{1... | collective-permute-start | bytes 196616 | tf_op jit(solution)/shard_map/ppermute | solution.py:501
  95.3 10.0 %collective-permute-start.9 = (f32[1,32,512]{2,1,0:T(8,128)S(1)}, f32[1,32,512]{2,1,0:T(8,128)S(1)}, u32[]{:S(2)}, u32[]{:S(2)}) collective-permute-start(f32[1,32,512]{2,1,0:T(8,128)S(1)} %get-tuple-element.88), channel_id=1, source_target_pairs={{0,16},{16,0},{32,48},{48,32},{64,80},{80,64},{96,112},{112,96},{1... | collective-permute-start | bytes 196616 | tf_op jit(solution)/shard_map/ppermute | solution.py:501
  100.7 6.9 %collective-permute-start.22 = (f32[384,128]{1,0:T(8,128)S(1)}, f32[384,128]{1,0:T(8,128)S(1)}, u32[]{:S(2)}, u32[]{:S(2)}) collective-permute-start(f32[384,128]{1,0:T(8,128)S(1)} %add.74.refs_4_), channel_id=1, source_target_pairs={{0,12},{16,20},{32,44},{48,52},{64,76},{80,84},{96,108},{112,116},... | collective-permute-start | bytes 589832 | tf_op jit(solution)/shard_map/ppermute | solution.py:517
  103.0 15.1 %collective-permute-start.17 = (f32[768,128]{1,0:T(8,128)S(1)}, f32[768,128]{1,0:T(8,128)S(1)}, u32[]{:S(2)}, u32[]{:S(2)}) collective-permute-start(f32[768,128]{1,0:T(8,128)S(1)} %pad_maximum_fusion), channel_id=1, source_target_pairs={{0,1},{16,19},{32,33},{48,51},{64,65},{80,83},{96,97},{112,115},{1... | collective-permute-start | bytes 1179656 | tf_op jit(solution)/shard_map/ppermute | solution.py:517
  103.1 13.0 %collective-permute-start.34 = (f32[256,128]{1,0:T(8,128)S(1)}, f32[256,128]{1,0:T(8,128)S(1)}, u32[]{:S(2)}, u32[]{:S(2)}) collective-permute-start(f32[256,128]{1,0:T(8,128)S(1)} %slice.114), channel_id=1, source_target_pairs={{0,1},{16,19},{32,33},{48,51},{64,65},{80,83},{96,97},{112,115},{1... | collective-permute-start | bytes 393224 | tf_op jit(solution)/shard_map/ppermute | solution.py:517
  105.2 12.9 %collective-permute-start.35 = (f32[360,128]{1,0:T(8,128)S(1)}, f32[360,128]{1,0:T(8,128)S(1)}, u32[]{:S(2)}, u32[]{:S(2)}) collective-permute-start(f32[360,128]{1,0:T(8,128)S(1)} %pad_maximum_fusion.4), channel_id=1, source_target_pairs={{0,1},{16,19},{32,33},{48,51},{64,65},{80,83},{96,97},{112,115},{1... | collective-permute-start | bytes 552968 | tf_op jit(solution)/shard_map/ppermute | solution.py:517
  105.3 12.8 %collective-permute-start.23 = (f32[384,128]{1,0:T(8,128)S(1)}, f32[384,128]{1,0:T(8,128)S(1)}, u32[]{:S(2)}, u32[]{:S(2)}) collective-permute-start(f32[384,128]{1,0:T(8,128)S(1)} %add.74.refs_4_), channel_id=1, source_target_pairs={{0,3},{16,17},{32,35},{48,49},{64,67},{80,81},{96,99},{112,113},{1... | collective-permute-start | bytes 589832 | tf_op jit(solution)/shard_map/ppermute | solution.py:517
  107.5 10.6 %collective-permute-start.24 = (f32[384,128]{1,0:T(8,128)S(1)}, f32[384,128]{1,0:T(8,128)S(1)}, u32[]{:S(2)}, u32[]{:S(2)}) collective-permute-start(f32[384,128]{1,0:T(8,128)S(1)} %collective-permute-done.22.refs_5_), channel_id=1, source_target_pairs={{0,3},{16,17},{32,35},{48,49},{64,67},{80,81},{96,99},{112,113},{1... | collective-permute-start | bytes 589832 | tf_op jit(solution)/shard_map/ppermute | solution.py:517
  (12 other events, 57.3 us)
